TPU v7x, 128 devices: a whole 4x4x4 slice. The times are simulated.
128 devices in a mesh: row: 64 (over y, z, x_lo, core), dir: 2 (over x_hi).
Axes of the slice: x: 4 (x_hi: 2, x_lo: 2; x = x_hi * 2 + x_lo), y: 4, z: 4, core: 2. Of those that a mesh axis runs over, the one named last changes fastest.
Arguments:
- incident: float32 [16384, 4096], P('row', 'dir'), may hold values from -6 to 6
- right_side: float32 [16384, 4096], P('row', 'dir'), may hold values from -6 to 6
- compress: float32 [16384, 128], P('row'), may hold values from -0.5 to 0.5
- level_diag: float32 [6, 128, 128, 128], P(None, 'row'), may hold values from -0.375 to 0.375
- level_cross: float32 [6, 128, 128, 128], P(None, 'row'), may hold values from -0.375 to 0.375
- expand: float32 [16384, 128], P('row'), may hold values from -0.5 to 0.5
- near_blocks: float32 [128, 8, 128, 128], P('row'), may hold values from -0.1875 to 0.1875
- near_cols: int32 [128, 8], P('row'), may hold values from 0 to 127, as said below
Outputs:
- residual: float32 [16384, 4096], P('row', 'dir')
- block_rms: float32 [128], P('row')
Inputs may be any that keep to these rules, and one draw needn't show every extreme that they name: `near_cols`: the entries of block row b lie between max(b - 2, 0) and min(b + 2, 127), and both ends are named in every block row; entries may repeat.
All inputs are finite; a program needn't handle non-finite values.
Results may differ from a plain program's by a relative error of at most 0.0001.
Values sent between devices are 32-bit elements; how exact they have to be, the bound alone decides.
No kernel may reach another device: no remote copies, remote signals or barrier semaphores. Data moves between devices by JAX's collectives and lax.ppermute only.
A program may use at most 128 MiB of HBM per device.

v0:
```python
import functools

import jax
import jax.numpy as jnp
from jax import lax
from jax.experimental import pallas as pl
from jax.experimental.pallas import tpu as pltpu
from jax.sharding import PartitionSpec as P


F32, BF16 = jnp.float32, jnp.bfloat16
WIDTHS = (256, 512, 512, 512, 256)
STARTS = (0, 512, 1024, 1536, 256)
EARLY = (0,)


def mm(a, b):
    return jnp.dot(a, b, precision=lax.Precision.HIGHEST, preferred_element_type=F32)


def split(x):
    high = x.astype(BF16)
    return high, (x - high.astype(F32)).astype(BF16)


def product(w, x):
    m = w.shape[0] // 2
    high, low = split(x)
    both = jnp.dot(w, high, preferred_element_type=F32)
    rest = jnp.dot(w[:m], low, preferred_element_type=F32)
    return both[:m] + both[m:] + rest


def put(ref, where, value):
    high, low = split(value)
    m = value.shape[0]
    ref[where + (slice(0, m),)] = high
    ref[where + (slice(m, 2 * m),)] = low


def cost(flops, size):
    return pl.CostEstimate(flops=flops, bytes_accessed=size, transcendentals=0)


def first_kernel(c, c1, d, x, out):
    b = c.shape[0] // 2
    nt = functools.partial(
        lax.dot_general,
        dimension_numbers=(((1,), (1,)), ((), ())),
        precision=lax.Precision.HIGHEST,
        preferred_element_type=F32,
    )
    for p in range(2):
        rows = slice(p * b, (p + 1) * b)
        out[p, :, :b] = nt(d[0, p], c[rows, :])
        out[p, :, b:] = nt(x[0, p], c1[rows, :])


def second_kernel(mine, other, d, x, out):
    for p in range(2):
        value = jnp.concatenate([mm(d[1, p], mine[p]), mm(x[1, p], other[p])], axis=1)
        put(out, (p,), value)


def radix4(even, d, x, o, level, p):
    d0, x0, d0o, x0o = d[level, p], x[level, p], o[0, p], o[1, p]
    d1, x1 = d[level + 1, p], x[level + 1, p]
    one, three = mm(d1, x0), mm(x1, x0o)
    return jnp.concatenate(
        [mm(d1, d0), jnp.where(even, one, three), jnp.where(even, three, one), mm(x1, d0o)], axis=1
    )


def third_kernel(place, d, x, o2, outz):
    for p in range(2):
        put(outz, (p,), radix4(place[1] == 0, d, x, o2, 2, p))


def fourth_kernel(place, d, x, o4, e, outy):
    b = e.shape[0] // 2
    for p in range(2):
        value = radix4(place[1] == 0, d, x, o4, 4, p)
        put(outy, (p,), mm(e[p * b : (p + 1) * b, :], value))


def near_weights_kernel(place, cols, blocks, out):
    i = place[0]
    odd = i % 2
    other = i + 1 - 2 * odd
    third = i - 1 + 2 * odd
    b = blocks.shape[-1]
    for p in range(2):
        for s, device in enumerate((i, other, third)):
            for q in range(2):
                wanted = 2 * device + q
                total = jnp.zeros((b, b), F32)
                for j in range(blocks.shape[1]):
                    total = total + jnp.where(cols[p, j] == wanted, blocks[p, j], 0.0)
                high, low = split(total)
                k = (2 * s + q) * b
                out[p * b : (p + 1) * b, k : k + b] = high
                out[(2 + p) * b : (3 + p) * b, k : k + b] = low


def stage_x_kernel(start, w, own, one, two, three, out):
    width = out.shape[1]
    b = out.shape[0] // 2
    for p in range(2):
        rows = slice(p * b, (p + 1) * b)
        x = jnp.concatenate(
            [own[rows, :], one[rows, start : start + width], two[rows, :], three[rows, :]], axis=0
        )
        out[rows, :] = product(w[p], x)


def stage_z_kernel(w, own, a, b, c, out):
    n = out.shape[0] // 2
    for p in range(2):
        rows = slice(p * n, (p + 1) * n)
        x = jnp.concatenate([ref[rows, :] for ref in (own, a, b, c)], axis=0)
        out[rows, :] = product(w[p], x)


def near_kernel(start, place, w, own, one, three, halo, right, out):
    here = slice(start, start + out.shape[1])
    third = jnp.where(place[2] == 1, halo[...], three[...])
    x = jnp.concatenate([own[...], one[:, here], third], axis=0)
    out[...] = right[:, here] - product(w[...], x)


def last_kernel(w, own, a, b, c, part, *refs):
    old_sum, out, total = refs[-3:]
    n = out.shape[0] // 2
    for p in range(2):
        rows = slice(p * n, (p + 1) * n)
        x = jnp.concatenate([ref[rows, :] for ref in (own, a, b, c)], axis=0)
        diff = part[rows, :] - product(w[p], x)
        out[rows, :] = diff
        total[p : p + 1, :] = old_sum[p : p + 1, :] + jnp.full((1, 128), jnp.sum(diff * diff), F32)


def xor(x, bits, odd_bits=None):
    count = lax.axis_size("row")
    odd_bits = bits if odd_bits is None else odd_bits
    return lax.ppermute(x, "row", [(i, i ^ (odd_bits if i % 2 else bits)) for i in range(count)])


def halo_of(x, two, early):
    count = lax.axis_size("row")
    if early:
        route = [(i, i + 1) for i in range(3, count - 1, 4)]
        return lax.ppermute(x, "row", route + [(j, i) for i, j in route])
    route = [(i, i + 3) for i in range(1, count - 3, 4)] + [(i, i - 3) for i in range(6, count, 4)]
    return lax.ppermute(two, "row", route)


VM = pl.BlockSpec(memory_space=pltpu.VMEM)
SM = pl.BlockSpec(memory_space=pltpu.SMEM)
ANY = pl.BlockSpec(memory_space=pl.ANY)


def call(kernel, in_specs, out_shape, flops, *args, limit=6, **kwargs):
    size = sum(a.size * a.dtype.itemsize for a in args)
    kwargs.setdefault("out_specs", VM)
    return pl.pallas_call(
        kernel,
        in_specs=in_specs,
        out_shape=out_shape,
        cost_estimate=cost(flops, size // 4),
        compiler_params=pltpu.CompilerParams(vmem_limit_bytes=limit * 2**20),
        **kwargs,
    )(*args)


def shards(incident, right_side, compress, level_diag, level_cross, expand, near_blocks, near_cols):
    rows, cols = incident.shape
    b = near_blocks.shape[2]
    i = lax.axis_index("row")
    quad = i % 4
    place = jnp.stack([i, i % 2, ((quad == 0) | (quad == 3)).astype(jnp.int32)]).astype(jnp.int32)
    shape = jax.ShapeDtypeStruct
    weights = shape((2, 2 * b, 4 * b), BF16)

    comp1 = xor(compress, 1)
    raw = [lax.slice_in_dim(incident, s, s + w, axis=1) for s, w in zip(STARTS, WIDTHS)]
    two = [xor(x, 2) for x in raw]
    one = xor(incident, 1)
    mine = call(
        first_kernel, [VM] * 4, shape((2, b, 2 * b), F32), 48 * b**3,
        compress, comp1, level_diag, level_cross,
    )
    ends = [(i * 2 + d, (i ^ 2) * 2 + 1 - d) for i in range(lax.axis_size("row")) for d in range(2)]
    theirs = lax.ppermute(mine, ("row", "dir"), ends)
    pair = lambda level: jnp.stack([level_diag[level], level_cross[level]])
    o2 = xor(pair(2), 8)
    o4 = xor(pair(4), 32)
    wx = call(second_kernel, [VM] * 4, weights, 96 * b**3, mine, theirs, level_diag, level_cross)
    wn = call(
        near_weights_kernel, [SM, SM, VM], shape((4 * b, 6 * b), BF16), 2**22,
        place, near_cols, near_blocks,
    )
    wz = call(third_kernel, [SM] + [VM] * 3, weights, 96 * b**3, place, level_diag, level_cross, o2)
    wy = call(
        fourth_kernel, [SM] + [VM] * 4, weights, 200 * b**3,
        place, level_diag, level_cross, o4, expand,
    )

    def gathered(x, near_bits, far_bits):
        a = xor(x, near_bits, far_bits)
        c = xor(x, far_bits, near_bits)
        return x, a, c, xor(a, far_bits, near_bits)

    result = None
    total = jnp.zeros((2, 128), F32)
    for k, (s, w) in enumerate(zip(STARTS, WIDTHS)):
        flops = 2 * 3 * 2 * 4 * b * b * w
        piece = shape((rows, w), F32)
        three = xor(two[k], 1)
        halo = halo_of(raw[k], two[k], k in EARLY)
        coeffs = call(functools.partial(stage_x_kernel, s), [VM] * 5, piece, flops, wx, raw[k], one, two[k], three)
        coeffs = call(stage_z_kernel, [VM] * 5, piece, flops, wz, *gathered(coeffs, 4, 12))
        part = call(
            functools.partial(near_kernel, s), [SM] + [VM] * 6, piece, 2 * flops,
            place, wn, raw[k], one, three, halo, right_side,
        )
        ins = gathered(coeffs, 16, 48)
        olds = () if result is None else (result,)
        out = pl.BlockSpec((rows, w), lambda j, s=s // w: (0, s))
        result, total = call(
            last_kernel, [VM] * 6 + [ANY] * len(olds) + [VM],
            [shape((rows, cols), F32), shape((2, 128), F32)], flops,
            wy, *ins, part, *olds, total,
            grid=(1,), out_specs=[out, VM],
            input_output_aliases={6: 0} if olds else {},
        )

    mate = lax.ppermute(total, "dir", [(0, 1), (1, 0)])
    mean = (total[:, 0] + mate[:, 0]) / (b * cols * lax.axis_size("dir"))
    return result, jnp.sqrt(mean + 1e-06)


def solution(mesh):
    return jax.shard_map(
        shards,
        mesh=mesh,
        in_specs=(
            P("row", "dir"),
            P("row", "dir"),
            P("row", None),
            P(None, "row", None, None),
            P(None, "row", None, None),
            P("row", None),
            P("row", None, None, None),
            P("row", None),
        ),
        out_specs=(P("row", "dir"), P("row")),
        check_vma=False,
    )
```

profile of v0, /device:TPU:14, one launch (start us, length us, event | category | flops | bytes accessed | tf_op | source)
XLA Modules:
  0.0 218.8 jit_solution(18404402166016865557)
XLA Ops:
  3.5 4.0 %collective-permute-start.2 = (f32[256,128]{1,0:T(8,128)}, f32[256,128]{1,0:T(8,128)S(1)}, u32[]{:S(2)}, u32[]{:S(2)}) collective-permute-start(f32[256,128]{1,0:T(8,128)} %c.1), channel_id=1, source_target_pairs={{0,2},{2,0},{4,6},{6,4},{8,10},{10,8},{12,14},{14,12},{16,18},{18,... | collective-permute-start | bytes 393224 | tf_op jit(solution)/shard_map/ppermute | solution.py:145
  8.7 3.7 %collective-permute-start.1 = (f32[2,2,128,128]{3,2,1,0:T(8,128)S(1)}, f32[2,2,128,128]{3,2,1,0:T(8,128)S(1)}, u32[]{:S(2)}, u32[]{:S(2)}) collective-permute-start(f32[2,2,128,128]{3,2,1,0:T(8,128)S(1)} %pad_maximum_fusion.1), channel_id=1, source_target_pairs={{0,16},{2,18},{4,20},{6,22},{8,24},{10,26},{12,28},{14,30},{16,0},... | collective-permute-start | bytes 786440 | tf_op jit(solution)/shard_map/ppermute | solution.py:145
  12.4 2.4 %collective-permute-start = (f32[2,2,128,128]{3,2,1,0:T(8,128)S(1)}, f32[2,2,128,128]{3,2,1,0:T(8,128)S(1)}, u32[]{:S(2)}, u32[]{:S(2)}) collective-permute-start(f32[2,2,128,128]{3,2,1,0:T(8,128)S(1)} %pad_maximum_fusion), channel_id=1, source_target_pairs={{0,64},{2,66},{4,68},{6,70},{8,72},{10,74},{12,76},{14,78},{16,80}... | collective-permute-start | bytes 786440 | tf_op jit(solution)/shard_map/ppermute | solution.py:145
  15.0 3.9 %collective-permute-done.1.o2 = f32[2,2,128,128]{3,2,1,0:T(8,128)S(1)} collective-permute-done((f32[2,2,128,128]{3,2,1,0:T(8,128)S(1)}, f32[2,2,128,128]{3,2,1,0:T(8,128)S(1)}, u32[]{:S(2)}, u32[]{:S(2)}) %collective-permute-start.1) | collective-permute-done | bytes 262176 | tf_op jit(solution)/shard_map/ppermute | solution.py:145
  18.9 4.4 %collective-permute-start.32 = (f32[256,512]{1,0:T(8,128)S(1)}, f32[256,512]{1,0:T(8,128)S(1)}, u32[]{:S(2)}, u32[]{:S(2)}) collective-permute-start(f32[256,512]{1,0:T(8,128)S(1)} %get-tuple-element.24.own), channel_id=1, source_target_pairs={{0,4},{2,6},{4,0},{6,2},{8,12},{10,14},{12,8},{14,10},{16,20},{18,... | collective-permute-start | bytes 1572872 | tf_op jit(solution)/shard_map/ppermute | solution.py:145
  26.8 14.9 %collective-permute-done.5.two = f32[256,256]{1,0:T(8,128)S(1)} collective-permute-done((f32[256,256]{1,0:T(8,128)S(1)}, f32[256,256]{1,0:T(8,128)S(1)}, u32[]{:S(2)}, u32[]{:S(2)}) %collective-permute-start.5) | collective-permute-done | bytes 262176 | tf_op jit(solution)/shard_map/ppermute | solution.py:145
  41.6 2.0 collective-permute-start.14
  45.3 7.5 %collective-permute-done.23.two = f32[256,512]{1,0:T(8,128)S(1)} collective-permute-done((f32[256,512]{1,0:T(8,128)S(1)}, f32[256,512]{1,0:T(8,128)S(1)}, u32[]{:S(2)}, u32[]{:S(2)}) %collective-permute-start.23) | collective-permute-done | bytes 524320 | tf_op jit(solution)/shard_map/ppermute | solution.py:145
  54.6 8.8 %collective-permute-done.14.two = f32[256,512]{1,0:T(8,128)S(1)} collective-permute-done((f32[256,512]{1,0:T(8,128)S(1)}, f32[256,512]{1,0:T(8,128)S(1)}, u32[]{:S(2)}, u32[]{:S(2)}) %collective-permute-start.14) | collective-permute-done | bytes 524320 | tf_op jit(solution)/shard_map/ppermute | solution.py:145
  63.4 2.5 %collective-permute-start.40 = (f32[256,512]{1,0:T(8,128)S(1)}, f32[256,512]{1,0:T(8,128)S(1)}, u32[]{:S(2)}, u32[]{:S(2)}) collective-permute-start(f32[256,512]{1,0:T(8,128)S(1)} %collective-permute-done.32.two), channel_id=1, source_target_pairs={{2,8},{10,16},{18,24},{26,32},{34,40},{42,48},{50,56},{58,64},{66,... | collective-permute-start | bytes 1572872 | tf_op jit(solution)/shard_map/ppermute | solution.py:154
  66.7 2.7 %collective-permute-start.31 = (f32[256,512]{1,0:T(8,128)S(1)}, f32[256,512]{1,0:T(8,128)S(1)}, u32[]{:S(2)}, u32[]{:S(2)}) collective-permute-start(f32[256,512]{1,0:T(8,128)S(1)} %collective-permute-done.23.two), channel_id=1, source_target_pairs={{2,8},{10,16},{18,24},{26,32},{34,40},{42,48},{50,56},{58,64},{66,... | collective-permute-start | bytes 1572872 | tf_op jit(solution)/shard_map/ppermute | solution.py:154
  69.6 3.6 %collective-permute-start.22 = (f32[256,512]{1,0:T(8,128)S(1)}, f32[256,512]{1,0:T(8,128)S(1)}, u32[]{:S(2)}, u32[]{:S(2)}) collective-permute-start(f32[256,512]{1,0:T(8,128)S(1)} %collective-permute-done.14.two), channel_id=1, source_target_pairs={{2,8},{10,16},{18,24},{26,32},{34,40},{42,48},{50,56},{58,64},{66,... | collective-permute-start | bytes 1572872 | tf_op jit(solution)/shard_map/ppermute | solution.py:154
  74.8 2.0 collective-permute-start.44
  78.7 4.7 %collective-permute-start.8 = (f32[256,256]{1,0:T(8,128)S(1)}, f32[256,256]{1,0:T(8,128)S(1)}, u32[]{:S(2)}, u32[]{:S(2)}) collective-permute-start(f32[256,256]{1,0:T(8,128)S(1)} %shard_map.99.own), channel_id=1, source_target_pairs={{0,24},{2,10},{4,28},{6,14},{8,16},{10,2},{12,20},{14,6},{16,8},{1... | collective-permute-start | bytes 786440 | tf_op jit(solution)/shard_map/ppermute | solution.py:145
  83.4 10.0 %collective-permute-done.43.a = f32[256,256]{1,0:T(8,128)S(1)} collective-permute-done((f32[256,256]{1,0:T(8,128)S(1)}, f32[256,256]{1,0:T(8,128)S(1)}, u32[]{:S(2)}, u32[]{:S(2)}) %collective-permute-start.43) | collective-permute-done | bytes 262176 | tf_op jit(solution)/shard_map/ppermute | solution.py:145
  96.4 1.8 collective-permute-start.35
  106.1 14.5 %collective-permute-done.9.c = f32[256,256]{1,0:T(8,128)S(1)} collective-permute-done((f32[256,256]{1,0:T(8,128)S(1)}, f32[256,256]{1,0:T(8,128)S(1)}, u32[]{:S(2)}, u32[]{:S(2)}) %collective-permute-start.9) | collective-permute-done | bytes 262176 | tf_op jit(solution)/shard_map/ppermute | solution.py:145
  135.3 2.4 %collective-permute-done.17.b = f32[256,512]{1,0:T(8,128)} collective-permute-done((f32[256,512]{1,0:T(8,128)}, f32[256,512]{1,0:T(8,128)}, u32[]{:S(2)}, u32[]{:S(2)}) %collective-permute-start.17) | collective-permute-done | bytes 524320 | tf_op jit(solution)/shard_map/ppermute | solution.py:145
  137.6 3.3 %collective-permute-start.47 = (f32[256,256]{1,0:T(8,128)S(1)}, f32[256,256]{1,0:T(8,128)S(1)}, u32[]{:S(2)}, u32[]{:S(2)}) collective-permute-start(f32[256,256]{1,0:T(8,128)S(1)} %shard_map.113.own), channel_id=1, source_target_pairs={{0,96},{2,34},{4,100},{6,38},{8,104},{10,42},{12,108},{14,46},{16,... | collective-permute-start | bytes 786440 | tf_op jit(solution)/shard_map/ppermute | solution.py:145
  140.9 2.3 %collective-permute-done.36.c = f32[256,512]{1,0:T(8,128)} collective-permute-done((f32[256,512]{1,0:T(8,128)}, f32[256,512]{1,0:T(8,128)}, u32[]{:S(2)}, u32[]{:S(2)}) %collective-permute-start.36) | collective-permute-done | bytes 524320 | tf_op jit(solution)/shard_map/ppermute | solution.py:145
  145.9 3.0 %collective-permute-done.27.c = f32[256,512]{1,0:T(8,128)} collective-permute-done((f32[256,512]{1,0:T(8,128)}, f32[256,512]{1,0:T(8,128)}, u32[]{:S(2)}, u32[]{:S(2)}) %collective-permute-start.27) | collective-permute-done | bytes 524320 | tf_op jit(solution)/shard_map/ppermute | solution.py:145
  149.1 2.1 shard_map.107.own
  151.3 3.2 %collective-permute-done.18.c = f32[256,512]{1,0:T(8,128)} collective-permute-done((f32[256,512]{1,0:T(8,128)}, f32[256,512]{1,0:T(8,128)}, u32[]{:S(2)}, u32[]{:S(2)}) %collective-permute-start.18) | collective-permute-done | bytes 524320 | tf_op jit(solution)/shard_map/ppermute | solution.py:145
  154.8 2.1 shard_map.104.own
  156.9 5.6 %collective-permute-start.38 = (f32[256,512]{1,0:T(8,128)S(1)}, f32[256,512]{1,0:T(8,128)S(1)}, u32[]{:S(2)}, u32[]{:S(2)}) collective-permute-start(f32[256,512]{1,0:T(8,128)S(1)} %shard_map.110.own), channel_id=1, source_target_pairs={{0,96},{2,34},{4,100},{6,38},{8,104},{10,42},{12,108},{14,46},{16,... | collective-permute-start | bytes 1572872 | tf_op jit(solution)/shard_map/ppermute | solution.py:145
  163.2 11.5 %collective-permute-done.48.c = f32[256,256]{1,0:T(8,128)S(1)} collective-permute-done((f32[256,256]{1,0:T(8,128)S(1)}, f32[256,256]{1,0:T(8,128)S(1)}, u32[]{:S(2)}, u32[]{:S(2)}) %collective-permute-start.48) | collective-permute-done | bytes 262176 | tf_op jit(solution)/shard_map/ppermute | solution.py:145
  178.7 5.8 %collective-permute-start.21 = (f32[256,512]{1,0:T(8,128)S(1)}, f32[256,512]{1,0:T(8,128)S(1)}, u32[]{:S(2)}, u32[]{:S(2)}) collective-permute-start(f32[256,512]{1,0:T(8,128)S(1)} %collective-permute-done.19.a), channel_id=1, source_target_pairs={{0,96},{2,34},{4,100},{6,38},{8,104},{10,42},{12,108},{14,46},{16,... | collective-permute-start | bytes 1572872 | tf_op jit(solution)/shard_map/ppermute | solution.py:145
  185.7 1.8 shard_map.95.w
  190.6 2.0 collective-permute-start.12
  200.7 5.6 %collective-permute-done.21.c = f32[256,512]{1,0:T(8,128)S(1)} collective-permute-done((f32[256,512]{1,0:T(8,128)S(1)}, f32[256,512]{1,0:T(8,128)S(1)}, u32[]{:S(2)}, u32[]{:S(2)}) %collective-permute-start.21) | collective-permute-done | bytes 524320 | tf_op jit(solution)/shard_map/ppermute | solution.py:145
  209.1 2.8 %collective-permute-done.12.c = f32[256,256]{1,0:T(8,128)S(1)} collective-permute-done((f32[256,256]{1,0:T(8,128)S(1)}, f32[256,256]{1,0:T(8,128)S(1)}, u32[]{:S(2)}, u32[]{:S(2)}) %collective-permute-start.12) | collective-permute-done | bytes 262176 | tf_op jit(solution)/shard_map/ppermute | solution.py:145
  214.4 3.7 %collective-permute-done.50 = f32[2,128]{1,0:T(2,128)S(1)} collective-permute-done((f32[2,128]{1,0:T(2,128)S(1)}, f32[2,128]{1,0:T(2,128)S(1)}, u32[]{:S(2)}, u32[]{:S(2)}) %collective-permute-start.50) | collective-permute-done | bytes 1056 | tf_op jit(solution)/shard_map/ppermute | solution.py:237
  (227 shorter events, 66.7 us)
Async XLA Ops:
  0.6 68.9 %collective-permute-start.4 = (f32[256,2048]{1,0:T(8,128)}, f32[256,2048]{1,0:T(8,128)S(1)}, u32[]{:S(2)}, u32[]{:S(2)}) collective-permute-start(f32[256,2048]{1,0:T(8,128)} %param.8), channel_id=1, source_target_pairs={{0,2},{2,0},{4,6},{6,4},{8,10},{10,8},{12,14},{14,12},{16,18},{18,... | collective-permute-start | bytes 6291464 | tf_op jit(solution)/shard_map/ppermute | solution.py:145
  2.0 21.3 %collective-permute-start.41 = (f32[256,256]{1,0:T(8,128)S(1)}, f32[256,256]{1,0:T(8,128)S(1)}, u32[]{:S(2)}, u32[]{:S(2)}) collective-permute-start(f32[256,256]{1,0:T(8,128)S(1)} %get-tuple-element.22.own), channel_id=1, source_target_pairs={{0,4},{2,6},{4,0},{6,2},{8,12},{10,14},{12,8},{14,10},{16,20},{18,... | collective-permute-start | bytes 786440 | tf_op jit(solution)/shard_map/ppermute | solution.py:145
  2.9 21.1 %collective-permute-start.49 = (f32[256,256]{1,0:T(8,128)S(1)}, f32[256,256]{1,0:T(8,128)S(1)}, u32[]{:S(2)}, u32[]{:S(2)}) collective-permute-start(f32[256,256]{1,0:T(8,128)S(1)} %get-tuple-element.22.own), channel_id=1, source_target_pairs={{6,8},{14,16},{22,24},{30,32},{38,40},{46,48},{54,56},{62,64},{70,... | collective-permute-start | bytes 786440 | tf_op jit(solution)/shard_map/ppermute | solution.py:152
  18.9 24.8 %collective-permute-start.32 = (f32[256,512]{1,0:T(8,128)S(1)}, f32[256,512]{1,0:T(8,128)S(1)}, u32[]{:S(2)}, u32[]{:S(2)}) collective-permute-start(f32[256,512]{1,0:T(8,128)S(1)} %get-tuple-element.24.own), channel_id=1, source_target_pairs={{0,4},{2,6},{4,0},{6,2},{8,12},{10,14},{12,8},{14,10},{16,20},{18,... | collective-permute-start | bytes 1572872 | tf_op jit(solution)/shard_map/ppermute | solution.py:145
  23.2 18.4 %collective-permute-start.5 = (f32[256,256]{1,0:T(8,128)S(1)}, f32[256,256]{1,0:T(8,128)S(1)}, u32[]{:S(2)}, u32[]{:S(2)}) collective-permute-start(f32[256,256]{1,0:T(8,128)S(1)} %get-tuple-element.23.own), channel_id=1, source_target_pairs={{0,4},{2,6},{4,0},{6,2},{8,12},{10,14},{12,8},{14,10},{16,20},{18,... | collective-permute-start | bytes 786440 | tf_op jit(solution)/shard_map/ppermute | solution.py:145
  24.0 19.6 %collective-permute-start.3 = (f32[2,128,256]{2,1,0:T(8,128)S(1)}, f32[2,128,256]{2,1,0:T(8,128)S(1)}, u32[]{:S(2)}, u32[]{:S(2)}) collective-permute-start(f32[2,128,256]{2,1,0:T(8,128)S(1)} %shard_map.97.mine), channel_id=1, source_target_pairs={{0,5},{1,4},{2,7},{3,6},{4,1},{5,0},{6,3},{7,2},{8,13},{9,12},{10,... | collective-permute-start | bytes 786440 | tf_op jit(solution)/shard_map/ppermute | solution.py:193
  26.4 26.5 %collective-permute-start.23 = (f32[256,512]{1,0:T(8,128)S(1)}, f32[256,512]{1,0:T(8,128)S(1)}, u32[]{:S(2)}, u32[]{:S(2)}) collective-permute-start(f32[256,512]{1,0:T(8,128)S(1)} %get-tuple-element.25.own), channel_id=1, source_target_pairs={{0,4},{2,6},{4,0},{6,2},{8,12},{10,14},{12,8},{14,10},{16,20},{18,... | collective-permute-start | bytes 1572872 | tf_op jit(solution)/shard_map/ppermute | solution.py:145
  41.6 21.8 %collective-permute-start.14 = (f32[256,512]{1,0:T(8,128)S(1)}, f32[256,512]{1,0:T(8,128)S(1)}, u32[]{:S(2)}, u32[]{:S(2)}) collective-permute-start(f32[256,512]{1,0:T(8,128)S(1)} %get-tuple-element.26.own), channel_id=1, source_target_pairs={{0,4},{2,6},{4,0},{6,2},{8,12},{10,14},{12,8},{14,10},{16,20},{18,... | collective-permute-start | bytes 1572872 | tf_op jit(solution)/shard_map/ppermute | solution.py:145
  43.7 25.8 %collective-permute-start.33 = (f32[256,512]{1,0:T(8,128)S(1)}, f32[256,512]{1,0:T(8,128)S(1)}, u32[]{:S(2)}, u32[]{:S(2)}) collective-permute-start(f32[256,512]{1,0:T(8,128)S(1)} %collective-permute-done.32.two), channel_id=1, source_target_pairs={{0,2},{2,0},{4,6},{6,4},{8,10},{10,8},{12,14},{14,12},{16,18},{18,... | collective-permute-start | bytes 1572872 | tf_op jit(solution)/shard_map/ppermute | solution.py:145
  45.2 20.7 %collective-permute-start.6 = (f32[256,256]{1,0:T(8,128)S(1)}, f32[256,256]{1,0:T(8,128)S(1)}, u32[]{:S(2)}, u32[]{:S(2)}) collective-permute-start(f32[256,256]{1,0:T(8,128)S(1)} %collective-permute-done.5.two), channel_id=1, source_target_pairs={{0,2},{2,0},{4,6},{6,4},{8,10},{10,8},{12,14},{14,12},{16,18},{18,... | collective-permute-start | bytes 786440 | tf_op jit(solution)/shard_map/ppermute | solution.py:145
  69.6 24.5 %collective-permute-start.22 = (f32[256,512]{1,0:T(8,128)S(1)}, f32[256,512]{1,0:T(8,128)S(1)}, u32[]{:S(2)}, u32[]{:S(2)}) collective-permute-start(f32[256,512]{1,0:T(8,128)S(1)} %collective-permute-done.14.two), channel_id=1, source_target_pairs={{2,8},{10,16},{18,24},{26,32},{34,40},{42,48},{50,56},{58,64},{66,... | collective-permute-start | bytes 1572872 | tf_op jit(solution)/shard_map/ppermute | solution.py:154
  74.3 19.1 %collective-permute-start.43 = (f32[256,256]{1,0:T(8,128)S(1)}, f32[256,256]{1,0:T(8,128)S(1)}, u32[]{:S(2)}, u32[]{:S(2)}) collective-permute-start(f32[256,256]{1,0:T(8,128)S(1)} %shard_map.112.own), channel_id=1, source_target_pairs={{0,8},{2,26},{4,12},{6,30},{8,0},{10,18},{12,4},{14,22},{16,24},{1... | collective-permute-start | bytes 786440 | tf_op jit(solution)/shard_map/ppermute | solution.py:145
  74.8 21.6 %collective-permute-start.44 = (f32[256,256]{1,0:T(8,128)S(1)}, f32[256,256]{1,0:T(8,128)S(1)}, u32[]{:S(2)}, u32[]{:S(2)}) collective-permute-start(f32[256,256]{1,0:T(8,128)S(1)} %shard_map.112.own), channel_id=1, source_target_pairs={{0,24},{2,10},{4,28},{6,14},{8,16},{10,2},{12,20},{14,6},{16,8},{1... | collective-permute-start | bytes 786440 | tf_op jit(solution)/shard_map/ppermute | solution.py:145
  78.2 21.3 %collective-permute-start.7 = (f32[256,256]{1,0:T(8,128)S(1)}, f32[256,256]{1,0:T(8,128)S(1)}, u32[]{:S(2)}, u32[]{:S(2)}) collective-permute-start(f32[256,256]{1,0:T(8,128)S(1)} %shard_map.99.own), channel_id=1, source_target_pairs={{0,8},{2,26},{4,12},{6,30},{8,0},{10,18},{12,4},{14,22},{16,24},{1... | collective-permute-start | bytes 786440 | tf_op jit(solution)/shard_map/ppermute | solution.py:145
  78.7 23.6 %collective-permute-start.8 = (f32[256,256]{1,0:T(8,128)S(1)}, f32[256,256]{1,0:T(8,128)S(1)}, u32[]{:S(2)}, u32[]{:S(2)}) collective-permute-start(f32[256,256]{1,0:T(8,128)S(1)} %shard_map.99.own), channel_id=1, source_target_pairs={{0,24},{2,10},{4,28},{6,14},{8,16},{10,2},{12,20},{14,6},{16,8},{1... | collective-permute-start | bytes 786440 | tf_op jit(solution)/shard_map/ppermute | solution.py:145
  94.9 28.1 %collective-permute-start.34 = (f32[256,512]{1,0:T(8,128)S(1)}, f32[256,512]{1,0:T(8,128)}, u32[]{:S(2)}, u32[]{:S(2)}) collective-permute-start(f32[256,512]{1,0:T(8,128)S(1)} %shard_map.109.own), channel_id=1, source_target_pairs={{0,8},{2,26},{4,12},{6,30},{8,0},{10,18},{12,4},{14,22},{16,24},{1... | collective-permute-start | bytes 1572872 | tf_op jit(solution)/shard_map/ppermute | solution.py:145
  96.4 28.2 %collective-permute-start.35 = (f32[256,512]{1,0:T(8,128)S(1)}, f32[256,512]{1,0:T(8,128)S(1)}, u32[]{:S(2)}, u32[]{:S(2)}) collective-permute-start(f32[256,512]{1,0:T(8,128)S(1)} %shard_map.109.own), channel_id=1, source_target_pairs={{0,24},{2,10},{4,28},{6,14},{8,16},{10,2},{12,20},{14,6},{16,8},{1... | collective-permute-start | bytes 1572872 | tf_op jit(solution)/shard_map/ppermute | solution.py:145
  99.6 27.4 %collective-permute-start.25 = (f32[256,512]{1,0:T(8,128)}, f32[256,512]{1,0:T(8,128)}, u32[]{:S(2)}, u32[]{:S(2)}) collective-permute-start(f32[256,512]{1,0:T(8,128)} %shard_map.106.own), channel_id=1, source_target_pairs={{0,8},{2,26},{4,12},{6,30},{8,0},{10,18},{12,4},{14,22},{16,24},{1... | collective-permute-start | bytes 1572872 | tf_op jit(solution)/shard_map/ppermute | solution.py:145
  103.1 26.0 %collective-permute-start.16 = (f32[256,512]{1,0:T(8,128)}, f32[256,512]{1,0:T(8,128)}, u32[]{:S(2)}, u32[]{:S(2)}) collective-permute-start(f32[256,512]{1,0:T(8,128)} %shard_map.103.own), channel_id=1, source_target_pairs={{0,8},{2,26},{4,12},{6,30},{8,0},{10,18},{12,4},{14,22},{16,24},{1... | collective-permute-start | bytes 1572872 | tf_op jit(solution)/shard_map/ppermute | solution.py:145
  127.0 21.9 %collective-permute-start.27 = (f32[256,512]{1,0:T(8,128)}, f32[256,512]{1,0:T(8,128)}, u32[]{:S(2)}, u32[]{:S(2)}) collective-permute-start(f32[256,512]{1,0:T(8,128)} %collective-permute-done.25.a), channel_id=1, source_target_pairs={{0,24},{2,10},{4,28},{6,14},{8,16},{10,2},{12,20},{14,6},{16,8},{1... | collective-permute-start | bytes 1572872 | tf_op jit(solution)/shard_map/ppermute | solution.py:145
  129.0 25.5 %collective-permute-start.18 = (f32[256,512]{1,0:T(8,128)}, f32[256,512]{1,0:T(8,128)}, u32[]{:S(2)}, u32[]{:S(2)}) collective-permute-start(f32[256,512]{1,0:T(8,128)} %collective-permute-done.16.a), channel_id=1, source_target_pairs={{0,24},{2,10},{4,28},{6,14},{8,16},{10,2},{12,20},{14,6},{16,8},{1... | collective-permute-start | bytes 1572872 | tf_op jit(solution)/shard_map/ppermute | solution.py:145
  134.7 22.2 %collective-permute-start.46 = (f32[256,256]{1,0:T(8,128)S(1)}, f32[256,256]{1,0:T(8,128)S(1)}, u32[]{:S(2)}, u32[]{:S(2)}) collective-permute-start(f32[256,256]{1,0:T(8,128)S(1)} %shard_map.113.own), channel_id=1, source_target_pairs={{0,32},{2,98},{4,36},{6,102},{8,40},{10,106},{12,44},{14,110},{16,... | collective-permute-start | bytes 786440 | tf_op jit(solution)/shard_map/ppermute | solution.py:145
  137.6 24.9 %collective-permute-start.47 = (f32[256,256]{1,0:T(8,128)S(1)}, f32[256,256]{1,0:T(8,128)S(1)}, u32[]{:S(2)}, u32[]{:S(2)}) collective-permute-start(f32[256,256]{1,0:T(8,128)S(1)} %shard_map.113.own), channel_id=1, source_target_pairs={{0,96},{2,34},{4,100},{6,38},{8,104},{10,42},{12,108},{14,46},{16,... | collective-permute-start | bytes 786440 | tf_op jit(solution)/shard_map/ppermute | solution.py:145
  143.2 19.9 %collective-permute-start.10 = (f32[256,256]{1,0:T(8,128)S(1)}, f32[256,256]{1,0:T(8,128)S(1)}, u32[]{:S(2)}, u32[]{:S(2)}) collective-permute-start(f32[256,256]{1,0:T(8,128)S(1)} %shard_map.100.own), channel_id=1, source_target_pairs={{0,32},{2,98},{4,36},{6,102},{8,40},{10,106},{12,44},{14,110},{16,... | collective-permute-start | bytes 786440 | tf_op jit(solution)/shard_map/ppermute | solution.py:145
  148.9 27.4 %collective-permute-start.37 = (f32[256,512]{1,0:T(8,128)S(1)}, f32[256,512]{1,0:T(8,128)S(1)}, u32[]{:S(2)}, u32[]{:S(2)}) collective-permute-start(f32[256,512]{1,0:T(8,128)S(1)} %shard_map.110.own), channel_id=1, source_target_pairs={{0,32},{2,98},{4,36},{6,102},{8,40},{10,106},{12,44},{14,110},{16,... | collective-permute-start | bytes 1572872 | tf_op jit(solution)/shard_map/ppermute | solution.py:145
  154.5 22.2 %collective-permute-start.28 = (f32[256,512]{1,0:T(8,128)S(1)}, f32[256,512]{1,0:T(8,128)S(1)}, u32[]{:S(2)}, u32[]{:S(2)}) collective-permute-start(f32[256,512]{1,0:T(8,128)S(1)} %shard_map.107.own), channel_id=1, source_target_pairs={{0,32},{2,98},{4,36},{6,102},{8,40},{10,106},{12,44},{14,110},{16,... | collective-permute-start | bytes 1572872 | tf_op jit(solution)/shard_map/ppermute | solution.py:145
  156.9 21.4 %collective-permute-start.38 = (f32[256,512]{1,0:T(8,128)S(1)}, f32[256,512]{1,0:T(8,128)S(1)}, u32[]{:S(2)}, u32[]{:S(2)}) collective-permute-start(f32[256,512]{1,0:T(8,128)S(1)} %shard_map.110.own), channel_id=1, source_target_pairs={{0,96},{2,34},{4,100},{6,38},{8,104},{10,42},{12,108},{14,46},{16,... | collective-permute-start | bytes 1572872 | tf_op jit(solution)/shard_map/ppermute | solution.py:145
  176.7 22.1 %collective-permute-start.30 = (f32[256,512]{1,0:T(8,128)S(1)}, f32[256,512]{1,0:T(8,128)S(1)}, u32[]{:S(2)}, u32[]{:S(2)}) collective-permute-start(f32[256,512]{1,0:T(8,128)S(1)} %collective-permute-done.28.a), channel_id=1, source_target_pairs={{0,96},{2,34},{4,100},{6,38},{8,104},{10,42},{12,108},{14,46},{16,... | collective-permute-start | bytes 1572872 | tf_op jit(solution)/shard_map/ppermute | solution.py:145
  178.3 22.4 %collective-permute-start.20 = (f32[256,512]{1,0:T(8,128)S(1)}, f32[256,512]{1,0:T(8,128)S(1)}, u32[]{:S(2)}, u32[]{:S(2)}) collective-permute-start(f32[256,512]{1,0:T(8,128)S(1)} %shard_map.104.own), channel_id=1, source_target_pairs={{0,96},{2,34},{4,100},{6,38},{8,104},{10,42},{12,108},{14,46},{16,... | collective-permute-start | bytes 1572872 | tf_op jit(solution)/shard_map/ppermute | solution.py:145
  178.7 27.6 %collective-permute-start.21 = (f32[256,512]{1,0:T(8,128)S(1)}, f32[256,512]{1,0:T(8,128)S(1)}, u32[]{:S(2)}, u32[]{:S(2)}) collective-permute-start(f32[256,512]{1,0:T(8,128)S(1)} %collective-permute-done.19.a), channel_id=1, source_target_pairs={{0,96},{2,34},{4,100},{6,38},{8,104},{10,42},{12,108},{14,46},{16,... | collective-permute-start | bytes 1572872 | tf_op jit(solution)/shard_map/ppermute | solution.py:145
  190.5 18.7 %collective-permute-start.11 = (f32[256,256]{1,0:T(8,128)S(1)}, f32[256,256]{1,0:T(8,128)S(1)}, u32[]{:S(2)}, u32[]{:S(2)}) collective-permute-start(f32[256,256]{1,0:T(8,128)S(1)} %shard_map.100.own), channel_id=1, source_target_pairs={{0,96},{2,34},{4,100},{6,38},{8,104},{10,42},{12,108},{14,46},{16,... | collective-permute-start | bytes 786440 | tf_op jit(solution)/shard_map/ppermute | solution.py:145
  190.6 21.4 %collective-permute-start.12 = (f32[256,256]{1,0:T(8,128)S(1)}, f32[256,256]{1,0:T(8,128)S(1)}, u32[]{:S(2)}, u32[]{:S(2)}) collective-permute-start(f32[256,256]{1,0:T(8,128)S(1)} %collective-permute-done.10.a), channel_id=1, source_target_pairs={{0,96},{2,34},{4,100},{6,38},{8,104},{10,42},{12,108},{14,46},{16,... | collective-permute-start | bytes 786440 | tf_op jit(solution)/shard_map/ppermute | solution.py:145
  (81 other events, 1247.5 us)
where the time goes:
time: 222 us; the launch traced here: 219 us
  waiting for transfers between devices  98.5 us (44%)
  starting transfers between devices  79 us (36%)
  Pallas kernels  28.8 us (13%)
  local copies, waits for them, and re-layouts  10.2 us (5%)
    ppermute x44, waiting for transfers between devices, xor(): lax.ppermute(x, 'row', [(i, i ^ (odd_bits if i % 2 else bits)) for i in r...  93.7 us
    ppermute x44, starting transfers between devices, xor(): lax.ppermute(x, 'row', [(i, i ^ (odd_bits if i % 2 else bits)) for i in r...  64.7 us
    pallas_call x25, Pallas kernels, call(): pl.pallas_call(kernel, in_specs=in_specs, out_shape=out_shape, cost_estim...  28.8 us
    ppermute x4, starting transfers between devices, halo_of(): return lax.ppermute(two, 'row', route)  10.6 us
    unnamed x124, local copies, waits for them, and re-layouts  7.67 us
  transfers between devices with their start and end apart: 51, of which 19 were waited for; matrix products, arithmetic and copies ran while one was open for 1% of the time, Pallas kernels for 13%

commit v1 on v0

--- a/solution.py
+++ b/solution.py
@@ -11,7 +11,6 @@
 F32, BF16 = jnp.float32, jnp.bfloat16
 WIDTHS = (256, 512, 512, 512, 256)
 STARTS = (0, 512, 1024, 1536, 256)
-EARLY = (0,)
 
 
 def mm(a, b):
@@ -40,6 +39,17 @@
 
 def cost(flops, size):
     return pl.CostEstimate(flops=flops, bytes_accessed=size, transcendentals=0)
+
+
+def copy_kernel(x, out):
+    out[...] = x[...]
+
+
+def pairs_kernel(d2, x2, d4, x4, out2, out4):
+    out2[0] = d2[0]
+    out2[1] = x2[0]
+    out4[0] = d4[0]
+    out4[1] = x4[0]
 
 
 def first_kernel(c, c1, d, x, out):
@@ -121,9 +131,9 @@
         out[rows, :] = product(w[p], x)
 
 
-def near_kernel(start, place, w, own, one, three, halo, right, out):
+def near_kernel(start, place, w, own, one, three, halo, cross, right, out):
     here = slice(start, start + out.shape[1])
-    third = jnp.where(place[2] == 1, halo[...], three[...])
+    third = jnp.where(place[2] == 1, halo[...] + cross[...], three[...])
     x = jnp.concatenate([own[...], one[:, here], third], axis=0)
     out[...] = right[:, here] - product(w[...], x)
 
@@ -145,13 +155,11 @@
     return lax.ppermute(x, "row", [(i, i ^ (odd_bits if i % 2 else bits)) for i in range(count)])
 
 
-def halo_of(x, two, early):
+def halo_of(two, crossing):
     count = lax.axis_size("row")
-    if early:
-        route = [(i, i + 1) for i in range(3, count - 1, 4)]
-        return lax.ppermute(x, "row", route + [(j, i) for i, j in route])
-    route = [(i, i + 3) for i in range(1, count - 3, 4)] + [(i, i - 3) for i in range(6, count, 4)]
-    return lax.ppermute(two, "row", route)
+    route = [(i, i + 3) for i in range(1, count - 3, 4)]
+    route = [(i, j) for i, j in route if (i // 16 != j // 16) == crossing]
+    return lax.ppermute(two, "row", route + [(j + 2, i + 2) for i, j in route])
 
 
 VM = pl.BlockSpec(memory_space=pltpu.VMEM)
@@ -182,7 +190,13 @@
     weights = shape((2, 2 * b, 4 * b), BF16)
 
     comp1 = xor(compress, 1)
-    raw = [lax.slice_in_dim(incident, s, s + w, axis=1) for s, w in zip(STARTS, WIDTHS)]
+    raw = [
+        call(
+            copy_kernel, [pl.BlockSpec((rows, w), lambda j, s=s // w: (0, s))],
+            shape((rows, w), F32), 0, incident, grid=(1,),
+        )
+        for s, w in zip(STARTS, WIDTHS)
+    ]
     two = [xor(x, 2) for x in raw]
     one = xor(incident, 1)
     mine = call(
@@ -191,9 +205,14 @@
     )
     ends = [(i * 2 + d, (i ^ 2) * 2 + 1 - d) for i in range(lax.axis_size("row")) for d in range(2)]
     theirs = lax.ppermute(mine, ("row", "dir"), ends)
-    pair = lambda level: jnp.stack([level_diag[level], level_cross[level]])
-    o2 = xor(pair(2), 8)
-    o4 = xor(pair(4), 32)
+    pairs = shape((2, 2, b, b), F32)
+    levels = [pl.BlockSpec((1, 2, b, b), lambda j, q=q: (q, 0, 0, 0)) for q in (2, 2, 4, 4)]
+    pair2, pair4 = call(
+        pairs_kernel, levels, [pairs, pairs], 0,
+        level_diag, level_cross, level_diag, level_cross, grid=(1,), out_specs=[VM, VM],
+    )
+    o2 = xor(pair2, 8)
+    o4 = xor(pair4, 32)
     wx = call(second_kernel, [VM] * 4, weights, 96 * b**3, mine, theirs, level_diag, level_cross)
     wn = call(
         near_weights_kernel, [SM, SM, VM], shape((4 * b, 6 * b), BF16), 2**22,
@@ -216,12 +235,13 @@
         flops = 2 * 3 * 2 * 4 * b * b * w
         piece = shape((rows, w), F32)
         three = xor(two[k], 1)
-        halo = halo_of(raw[k], two[k], k in EARLY)
+        halo = halo_of(two[k], False)
+        cross = halo_of(two[k], True)
         coeffs = call(functools.partial(stage_x_kernel, s), [VM] * 5, piece, flops, wx, raw[k], one, two[k], three)
         coeffs = call(stage_z_kernel, [VM] * 5, piece, flops, wz, *gathered(coeffs, 4, 12))
         part = call(
-            functools.partial(near_kernel, s), [SM] + [VM] * 6, piece, 2 * flops,
-            place, wn, raw[k], one, three, halo, right_side,
+            functools.partial(near_kernel, s), [SM] + [VM] * 7, piece, 2 * flops,
+            place, wn, raw[k], one, three, halo, cross, right_side,
         )
         ins = gathered(coeffs, 16, 48)
         olds = () if result is None else (result,)

time: 222 us -> 218 us (0.982)
  waiting for transfers between devices: 98.5 us -> 94.3 us
  starting transfers between devices: 79 us -> 75.7 us
  local copies, waits for them, and re-layouts: 10.2 us -> 13.1 us
    ppermute x44, waiting for transfers between devices: 93.7 us -> 84.8 us  [xor(): lax.ppermute(x, 'row', [(i, i ^ (odd_bits if i % 2 else bits)) for i in r...]
    ppermute x44, starting transfers between devices: 64.7 us -> 57.2 us  [xor(): lax.ppermute(x, 'row', [(i, i ^ (odd_bits if i % 2 else bits)) for i in r...]
    ppermute x5 -> x10, starting transfers between devices: 11.2 us -> 16.6 us  [halo_of(): return lax.ppermute(two, 'row', route + [(j + 2, i + 2) for i, j in route])]
    unnamed x124 -> x146, local copies, waits for them, and re-layouts: 7.67 us -> 13.1 us
    ppermute x5 -> x10, waiting for transfers between devices: 1.1 us -> 5.03 us  [halo_of(): return lax.ppermute(two, 'row', route + [(j + 2, i + 2) for i, j in route])]
    slice x3 -> x0, local copies, waits for them, and re-layouts: 2.49 us -> none  [the longest x2 1.36 us: shards(): lax.slice_in_dim(incident, s, s + w, axis=1)]
    pallas_call x25 -> x31, Pallas kernels: 28.8 us -> 29.1 us  [call(): pl.pallas_call(kernel, in_specs=in_specs, out_shape=out_shape, cost_estim...]
  transfers between devices with their start and end apart: 51 -> 56, of which waited for: 19 -> 24; matrix products, arithmetic and copies ran while one was open for 1% -> 0% of each run, Pallas kernels for 13% -> 13%
where the time goes in v1:
time: 218 us; the launch traced here: 215 us
  waiting for transfers between devices  94.3 us (43%)
  starting transfers between devices  75.7 us (35%)
  Pallas kernels  29.1 us (13%)
  local copies, waits for them, and re-layouts  13.1 us (6%)
    ppermute x44, waiting for transfers between devices, xor(): lax.ppermute(x, 'row', [(i, i ^ (odd_bits if i % 2 else bits)) for i in r...  84.8 us
    ppermute x44, starting transfers between devices, xor(): lax.ppermute(x, 'row', [(i, i ^ (odd_bits if i % 2 else bits)) for i in r...  57.2 us
    pallas_call x31, Pallas kernels, call(): pl.pallas_call(kernel, in_specs=in_specs, out_shape=out_shape, cost_estim...  29.1 us
    ppermute x10, starting transfers between devices, halo_of(): return lax.ppermute(two, 'row', route + [(j + 2, i + 2) for i, j in route])  16.6 us
    unnamed x146, local copies, waits for them, and re-layouts  13.1 us
    ppermute x10, waiting for transfers between devices, halo_of(): return lax.ppermute(two, 'row', route + [(j + 2, i + 2) for i, j in route])  5.03 us
  transfers between devices with their start and end apart: 56, of which 24 were waited for; matrix products, arithmetic and copies ran while one was open for 0% of the time, Pallas kernels for 13%

profile of v1, /device:TPU:14, one launch (start us, length us, event | category | flops | bytes accessed | tf_op | source)
XLA Modules:
  0.0 214.6 jit_solution(1513478539005434827)
XLA Ops:
  3.6 4.0 %collective-permute-start.1 = (f32[2,2,128,128]{3,2,1,0:T(8,128)S(1)}, f32[2,2,128,128]{3,2,1,0:T(8,128)S(1)}, u32[]{:S(2)}, u32[]{:S(2)}) collective-permute-start(f32[2,2,128,128]{3,2,1,0:T(8,128)S(1)} %get-tuple-element.15), channel_id=1, source_target_pairs={{0,16},{2,18},{4,20},{6,22},{8,24},{10,26},{12,28},{14,30},{16,0},... | collective-permute-start | bytes 786440 | tf_op jit(solution)/shard_map/ppermute | solution.py:155
  8.5 2.3 %collective-permute-start = (f32[2,2,128,128]{3,2,1,0:T(8,128)S(1)}, f32[2,2,128,128]{3,2,1,0:T(8,128)S(1)}, u32[]{:S(2)}, u32[]{:S(2)}) collective-permute-start(f32[2,2,128,128]{3,2,1,0:T(8,128)S(1)} %get-tuple-element.14), channel_id=1, source_target_pairs={{0,64},{2,66},{4,68},{6,70},{8,72},{10,74},{12,76},{14,78},{16,80}... | collective-permute-start | bytes 786440 | tf_op jit(solution)/shard_map/ppermute | solution.py:155
  14.5 2.3 %collective-permute-done.45.two = f32[256,256]{1,0:T(8,128)S(1)} collective-permute-done((f32[256,256]{1,0:T(8,128)S(1)}, f32[256,256]{1,0:T(8,128)S(1)}, u32[]{:S(2)}, u32[]{:S(2)}) %collective-permute-start.45) | collective-permute-done | bytes 262176 | tf_op jit(solution)/shard_map/ppermute | solution.py:155
  18.4 2.8 %collective-permute-done.5.two = f32[256,256]{1,0:T(8,128)S(1)} collective-permute-done((f32[256,256]{1,0:T(8,128)S(1)}, f32[256,256]{1,0:T(8,128)S(1)}, u32[]{:S(2)}, u32[]{:S(2)}) %collective-permute-start.5) | collective-permute-done | bytes 262176 | tf_op jit(solution)/shard_map/ppermute | solution.py:155
  25.8 2.3 %collective-permute-start.54 = (f32[256,256]{1,0:T(8,128)S(1)}, f32[256,256]{1,0:T(8,128)S(1)}, u32[]{:S(2)}, u32[]{:S(2)}) collective-permute-start(f32[256,256]{1,0:T(8,128)S(1)} %collective-permute-done.45.two), channel_id=1, source_target_pairs={{26,32},{58,64},{90,96},{36,30},{68,62},{100,94},{27,33},{59,65},{... | collective-permute-start | bytes 786440 | tf_op jit(solution)/shard_map/ppermute | solution.py:162
  28.2 3.9 %collective-permute-done.54.cross = f32[256,256]{1,0:T(8,128)S(1)} collective-permute-done((f32[256,256]{1,0:T(8,128)S(1)}, f32[256,256]{1,0:T(8,128)S(1)}, u32[]{:S(2)}, u32[]{:S(2)}) %collective-permute-start.54) | collective-permute-done | bytes 262176 | tf_op jit(solution)/shard_map/ppermute | solution.py:162
  32.7 3.3 %collective-permute-done.35.two = f32[256,512]{1,0:T(8,128)S(1)} collective-permute-done((f32[256,512]{1,0:T(8,128)S(1)}, f32[256,512]{1,0:T(8,128)S(1)}, u32[]{:S(2)}, u32[]{:S(2)}) %collective-permute-start.35) | collective-permute-done | bytes 524320 | tf_op jit(solution)/shard_map/ppermute | solution.py:155
  36.7 10.6 %collective-permute-done.25.two = f32[256,512]{1,0:T(8,128)S(1)} collective-permute-done((f32[256,512]{1,0:T(8,128)S(1)}, f32[256,512]{1,0:T(8,128)S(1)}, u32[]{:S(2)}, u32[]{:S(2)}) %collective-permute-start.25) | collective-permute-done | bytes 524320 | tf_op jit(solution)/shard_map/ppermute | solution.py:155
  48.6 8.1 %collective-permute-done.15.two = f32[256,512]{1,0:T(8,128)S(1)} collective-permute-done((f32[256,512]{1,0:T(8,128)S(1)}, f32[256,512]{1,0:T(8,128)S(1)}, u32[]{:S(2)}, u32[]{:S(2)}) %collective-permute-start.15) | collective-permute-done | bytes 524320 | tf_op jit(solution)/shard_map/ppermute | solution.py:155
  58.1 2.4 %collective-permute-start.44 = (f32[256,512]{1,0:T(8,128)S(1)}, f32[256,512]{1,0:T(8,128)S(1)}, u32[]{:S(2)}, u32[]{:S(2)}) collective-permute-start(f32[256,512]{1,0:T(8,128)S(1)} %collective-permute-done.35.two), channel_id=1, source_target_pairs={{26,32},{58,64},{90,96},{36,30},{68,62},{100,94},{27,33},{59,65},{... | collective-permute-start | bytes 1572872 | tf_op jit(solution)/shard_map/ppermute | solution.py:162
  62.8 3.2 %collective-permute-start.34 = (f32[256,512]{1,0:T(8,128)S(1)}, f32[256,512]{1,0:T(8,128)S(1)}, u32[]{:S(2)}, u32[]{:S(2)}) collective-permute-start(f32[256,512]{1,0:T(8,128)S(1)} %collective-permute-done.25.two), channel_id=1, source_target_pairs={{26,32},{58,64},{90,96},{36,30},{68,62},{100,94},{27,33},{59,65},{... | collective-permute-start | bytes 1572872 | tf_op jit(solution)/shard_map/ppermute | solution.py:162
  70.7 4.0 %collective-permute-start.24 = (f32[256,512]{1,0:T(8,128)S(1)}, f32[256,512]{1,0:T(8,128)S(1)}, u32[]{:S(2)}, u32[]{:S(2)}) collective-permute-start(f32[256,512]{1,0:T(8,128)S(1)} %collective-permute-done.15.two), channel_id=1, source_target_pairs={{26,32},{58,64},{90,96},{36,30},{68,62},{100,94},{27,33},{59,65},{... | collective-permute-start | bytes 1572872 | tf_op jit(solution)/shard_map/ppermute | solution.py:162
  78.3 4.9 %collective-permute-start.8 = (f32[256,256]{1,0:T(8,128)S(1)}, f32[256,256]{1,0:T(8,128)S(1)}, u32[]{:S(2)}, u32[]{:S(2)}) collective-permute-start(f32[256,256]{1,0:T(8,128)S(1)} %shard_map.101.own), channel_id=1, source_target_pairs={{0,24},{2,10},{4,28},{6,14},{8,16},{10,2},{12,20},{14,6},{16,8},{1... | collective-permute-start | bytes 786440 | tf_op jit(solution)/shard_map/ppermute | solution.py:155
  83.2 3.1 %collective-permute-done.47.a = f32[256,256]{1,0:T(8,128)S(1)} collective-permute-done((f32[256,256]{1,0:T(8,128)S(1)}, f32[256,256]{1,0:T(8,128)S(1)}, u32[]{:S(2)}, u32[]{:S(2)}) %collective-permute-start.47) | collective-permute-done | bytes 262176 | tf_op jit(solution)/shard_map/ppermute | solution.py:155
  89.6 2.8 %collective-permute-start.38 = (f32[256,512]{1,0:T(8,128)S(1)}, f32[256,512]{1,0:T(8,128)S(1)}, u32[]{:S(2)}, u32[]{:S(2)}) collective-permute-start(f32[256,512]{1,0:T(8,128)S(1)} %shard_map.114.own), channel_id=1, source_target_pairs={{0,24},{2,10},{4,28},{6,14},{8,16},{10,2},{12,20},{14,6},{16,8},{1... | collective-permute-start | bytes 1572872 | tf_op jit(solution)/shard_map/ppermute | solution.py:155
  96.1 2.0 collective-permute-start.17
  100.0 3.7 %collective-permute-start.9 = (f32[256,256]{1,0:T(8,128)S(1)}, f32[256,256]{1,0:T(8,128)S(1)}, u32[]{:S(2)}, u32[]{:S(2)}) collective-permute-start(f32[256,256]{1,0:T(8,128)S(1)} %collective-permute-done.7.a), channel_id=1, source_target_pairs={{0,24},{2,10},{4,28},{6,14},{8,16},{10,2},{12,20},{14,6},{16,8},{1... | collective-permute-start | bytes 786440 | tf_op jit(solution)/shard_map/ppermute | solution.py:155
  103.7 12.4 %collective-permute-done.9.c = f32[256,256]{1,0:T(8,128)S(1)} collective-permute-done((f32[256,256]{1,0:T(8,128)S(1)}, f32[256,256]{1,0:T(8,128)S(1)}, u32[]{:S(2)}, u32[]{:S(2)}) %collective-permute-start.9) | collective-permute-done | bytes 262176 | tf_op jit(solution)/shard_map/ppermute | solution.py:155
  116.8 3.7 %collective-permute-start.28 = (f32[256,512]{1,0:T(8,128)}, f32[256,512]{1,0:T(8,128)}, u32[]{:S(2)}, u32[]{:S(2)}) collective-permute-start(f32[256,512]{1,0:T(8,128)} %shard_map.110.own), channel_id=1, source_target_pairs={{0,24},{2,10},{4,28},{6,14},{8,16},{10,2},{12,20},{14,6},{16,8},{1... | collective-permute-start | bytes 1572872 | tf_op jit(solution)/shard_map/ppermute | solution.py:155
  121.4 3.2 %collective-permute-start.39 = (f32[256,512]{1,0:T(8,128)}, f32[256,512]{1,0:T(8,128)}, u32[]{:S(2)}, u32[]{:S(2)}) collective-permute-start(f32[256,512]{1,0:T(8,128)} %collective-permute-done.37.a), channel_id=1, source_target_pairs={{0,24},{2,10},{4,28},{6,14},{8,16},{10,2},{12,20},{14,6},{16,8},{1... | collective-permute-start | bytes 1572872 | tf_op jit(solution)/shard_map/ppermute | solution.py:155
  124.6 3.2 %collective-permute-start.19 = (f32[256,512]{1,0:T(8,128)}, f32[256,512]{1,0:T(8,128)}, u32[]{:S(2)}, u32[]{:S(2)}) collective-permute-start(f32[256,512]{1,0:T(8,128)} %collective-permute-done.17.a), channel_id=1, source_target_pairs={{0,24},{2,10},{4,28},{6,14},{8,16},{10,2},{12,20},{14,6},{16,8},{1... | collective-permute-start | bytes 1572872 | tf_op jit(solution)/shard_map/ppermute | solution.py:155
  135.2 4.0 %collective-permute-done.39.c = f32[256,512]{1,0:T(8,128)} collective-permute-done((f32[256,512]{1,0:T(8,128)}, f32[256,512]{1,0:T(8,128)}, u32[]{:S(2)}, u32[]{:S(2)}) %collective-permute-start.39) | collective-permute-done | bytes 524320 | tf_op jit(solution)/shard_map/ppermute | solution.py:155
  141.5 3.4 %collective-permute-done.29.c = f32[256,512]{1,0:T(8,128)} collective-permute-done((f32[256,512]{1,0:T(8,128)}, f32[256,512]{1,0:T(8,128)}, u32[]{:S(2)}, u32[]{:S(2)}) %collective-permute-start.29) | collective-permute-done | bytes 524320 | tf_op jit(solution)/shard_map/ppermute | solution.py:155
  145.3 2.1 shard_map.111.own
  147.4 3.0 %collective-permute-done.19.c = f32[256,512]{1,0:T(8,128)} collective-permute-done((f32[256,512]{1,0:T(8,128)}, f32[256,512]{1,0:T(8,128)}, u32[]{:S(2)}, u32[]{:S(2)}) %collective-permute-start.19) | collective-permute-done | bytes 524320 | tf_op jit(solution)/shard_map/ppermute | solution.py:155
  150.9 2.1 shard_map.107.own
  154.3 2.6 %collective-permute-start.20 = (f32[256,512]{1,0:T(8,128)S(1)}, f32[256,512]{1,0:T(8,128)S(1)}, u32[]{:S(2)}, u32[]{:S(2)}) collective-permute-start(f32[256,512]{1,0:T(8,128)S(1)} %shard_map.107.own), channel_id=1, source_target_pairs={{0,32},{2,98},{4,36},{6,102},{8,40},{10,106},{12,44},{14,110},{16,... | collective-permute-start | bytes 1572872 | tf_op jit(solution)/shard_map/ppermute | solution.py:155
  157.4 13.2 %collective-permute-done.52.c = f32[256,256]{1,0:T(8,128)S(1)} collective-permute-done((f32[256,256]{1,0:T(8,128)S(1)}, f32[256,256]{1,0:T(8,128)S(1)}, u32[]{:S(2)}, u32[]{:S(2)}) %collective-permute-start.52) | collective-permute-done | bytes 262176 | tf_op jit(solution)/shard_map/ppermute | solution.py:155
  182.7 2.6 %collective-permute-done.42.c = f32[256,512]{1,0:T(8,128)S(1)} collective-permute-done((f32[256,512]{1,0:T(8,128)S(1)}, f32[256,512]{1,0:T(8,128)S(1)}, u32[]{:S(2)}, u32[]{:S(2)}) %collective-permute-start.42) | collective-permute-done | bytes 524320 | tf_op jit(solution)/shard_map/ppermute | solution.py:155
  196.6 5.6 %collective-permute-done.22.c = f32[256,512]{1,0:T(8,128)S(1)} collective-permute-done((f32[256,512]{1,0:T(8,128)S(1)}, f32[256,512]{1,0:T(8,128)S(1)}, u32[]{:S(2)}, u32[]{:S(2)}) %collective-permute-start.22) | collective-permute-done | bytes 524320 | tf_op jit(solution)/shard_map/ppermute | solution.py:155
  205.0 2.8 %collective-permute-done.12.c = f32[256,256]{1,0:T(8,128)S(1)} collective-permute-done((f32[256,256]{1,0:T(8,128)S(1)}, f32[256,256]{1,0:T(8,128)S(1)}, u32[]{:S(2)}, u32[]{:S(2)}) %collective-permute-start.12) | collective-permute-done | bytes 262176 | tf_op jit(solution)/shard_map/ppermute | solution.py:155
  210.3 3.7 %collective-permute-done.55 = f32[2,128]{1,0:T(2,128)S(1)} collective-permute-done((f32[2,128]{1,0:T(2,128)S(1)}, f32[2,128]{1,0:T(2,128)S(1)}, u32[]{:S(2)}, u32[]{:S(2)}) %collective-permute-start.55) | collective-permute-done | bytes 1056 | tf_op jit(solution)/shard_map/ppermute | solution.py:257
  (260 shorter events, 79.7 us)
Async XLA Ops:
  0.6 70.0 %collective-permute-start.4 = (f32[256,2048]{1,0:T(8,128)}, f32[256,2048]{1,0:T(8,128)S(1)}, u32[]{:S(2)}, u32[]{:S(2)}) collective-permute-start(f32[256,2048]{1,0:T(8,128)} %x.17), channel_id=1, source_target_pairs={{0,2},{2,0},{4,6},{6,4},{8,10},{10,8},{12,14},{14,12},{16,18},{18,... | collective-permute-start | bytes 6291464 | tf_op jit(solution)/shard_map/ppermute | solution.py:155
  21.3 14.8 %collective-permute-start.35 = (f32[256,512]{1,0:T(8,128)S(1)}, f32[256,512]{1,0:T(8,128)S(1)}, u32[]{:S(2)}, u32[]{:S(2)}) collective-permute-start(f32[256,512]{1,0:T(8,128)S(1)} %shard_map.113.own), channel_id=1, source_target_pairs={{0,4},{2,6},{4,0},{6,2},{8,12},{10,14},{12,8},{14,10},{16,20},{18,... | collective-permute-start | bytes 1572872 | tf_op jit(solution)/shard_map/ppermute | solution.py:155
  23.0 24.3 %collective-permute-start.25 = (f32[256,512]{1,0:T(8,128)S(1)}, f32[256,512]{1,0:T(8,128)S(1)}, u32[]{:S(2)}, u32[]{:S(2)}) collective-permute-start(f32[256,512]{1,0:T(8,128)S(1)} %shard_map.109.own), channel_id=1, source_target_pairs={{0,4},{2,6},{4,0},{6,2},{8,12},{10,14},{12,8},{14,10},{16,20},{18,... | collective-permute-start | bytes 1572872 | tf_op jit(solution)/shard_map/ppermute | solution.py:155
  23.5 33.2 %collective-permute-start.15 = (f32[256,512]{1,0:T(8,128)S(1)}, f32[256,512]{1,0:T(8,128)S(1)}, u32[]{:S(2)}, u32[]{:S(2)}) collective-permute-start(f32[256,512]{1,0:T(8,128)S(1)} %shard_map.105.own), channel_id=1, source_target_pairs={{0,4},{2,6},{4,0},{6,2},{8,12},{10,14},{12,8},{14,10},{16,20},{18,... | collective-permute-start | bytes 1572872 | tf_op jit(solution)/shard_map/ppermute | solution.py:155
  32.7 23.9 %collective-permute-start.6 = (f32[256,256]{1,0:T(8,128)S(1)}, f32[256,256]{1,0:T(8,128)S(1)}, u32[]{:S(2)}, u32[]{:S(2)}) collective-permute-start(f32[256,256]{1,0:T(8,128)S(1)} %collective-permute-done.5.two), channel_id=1, source_target_pairs={{0,2},{2,0},{4,6},{6,4},{8,10},{10,8},{12,14},{14,12},{16,18},{18,... | collective-permute-start | bytes 786440 | tf_op jit(solution)/shard_map/ppermute | solution.py:155
  36.1 21.3 %collective-permute-start.13 = (f32[256,256]{1,0:T(8,128)S(1)}, f32[256,256]{1,0:T(8,128)S(1)}, u32[]{:S(2)}, u32[]{:S(2)}) collective-permute-start(f32[256,256]{1,0:T(8,128)S(1)} %collective-permute-done.5.two), channel_id=1, source_target_pairs={{2,8},{10,16},{18,24},{34,40},{42,48},{50,56},{66,72},{74,80},{82,... | collective-permute-start | bytes 786440 | tf_op jit(solution)/shard_map/ppermute | solution.py:162
  61.3 14.4 %collective-permute-start.33 = (f32[256,512]{1,0:T(8,128)S(1)}, f32[256,512]{1,0:T(8,128)S(1)}, u32[]{:S(2)}, u32[]{:S(2)}) collective-permute-start(f32[256,512]{1,0:T(8,128)S(1)} %collective-permute-done.25.two), channel_id=1, source_target_pairs={{2,8},{10,16},{18,24},{34,40},{42,48},{50,56},{66,72},{74,80},{82,... | collective-permute-start | bytes 1572872 | tf_op jit(solution)/shard_map/ppermute | solution.py:162
  70.7 16.3 %collective-permute-start.24 = (f32[256,512]{1,0:T(8,128)S(1)}, f32[256,512]{1,0:T(8,128)S(1)}, u32[]{:S(2)}, u32[]{:S(2)}) collective-permute-start(f32[256,512]{1,0:T(8,128)S(1)} %collective-permute-done.15.two), channel_id=1, source_target_pairs={{26,32},{58,64},{90,96},{36,30},{68,62},{100,94},{27,33},{59,65},{... | collective-permute-start | bytes 1572872 | tf_op jit(solution)/shard_map/ppermute | solution.py:162
  77.2 16.6 %collective-permute-start.7 = (f32[256,256]{1,0:T(8,128)S(1)}, f32[256,256]{1,0:T(8,128)S(1)}, u32[]{:S(2)}, u32[]{:S(2)}) collective-permute-start(f32[256,256]{1,0:T(8,128)S(1)} %shard_map.101.own), channel_id=1, source_target_pairs={{0,8},{2,26},{4,12},{6,30},{8,0},{10,18},{12,4},{14,22},{16,24},{1... | collective-permute-start | bytes 786440 | tf_op jit(solution)/shard_map/ppermute | solution.py:155
  78.3 17.0 %collective-permute-start.8 = (f32[256,256]{1,0:T(8,128)S(1)}, f32[256,256]{1,0:T(8,128)S(1)}, u32[]{:S(2)}, u32[]{:S(2)}) collective-permute-start(f32[256,256]{1,0:T(8,128)S(1)} %shard_map.101.own), channel_id=1, source_target_pairs={{0,24},{2,10},{4,28},{6,14},{8,16},{10,2},{12,20},{14,6},{16,8},{1... | collective-permute-start | bytes 786440 | tf_op jit(solution)/shard_map/ppermute | solution.py:155
  87.0 33.5 %collective-permute-start.37 = (f32[256,512]{1,0:T(8,128)S(1)}, f32[256,512]{1,0:T(8,128)}, u32[]{:S(2)}, u32[]{:S(2)}) collective-permute-start(f32[256,512]{1,0:T(8,128)S(1)} %shard_map.114.own), channel_id=1, source_target_pairs={{0,8},{2,26},{4,12},{6,30},{8,0},{10,18},{12,4},{14,22},{16,24},{1... | collective-permute-start | bytes 1572872 | tf_op jit(solution)/shard_map/ppermute | solution.py:155
  89.6 30.9 %collective-permute-start.38 = (f32[256,512]{1,0:T(8,128)S(1)}, f32[256,512]{1,0:T(8,128)S(1)}, u32[]{:S(2)}, u32[]{:S(2)}) collective-permute-start(f32[256,512]{1,0:T(8,128)S(1)} %shard_map.114.own), channel_id=1, source_target_pairs={{0,24},{2,10},{4,28},{6,14},{8,16},{10,2},{12,20},{14,6},{16,8},{1... | collective-permute-start | bytes 1572872 | tf_op jit(solution)/shard_map/ppermute | solution.py:155
  93.9 30.7 %collective-permute-start.27 = (f32[256,512]{1,0:T(8,128)}, f32[256,512]{1,0:T(8,128)}, u32[]{:S(2)}, u32[]{:S(2)}) collective-permute-start(f32[256,512]{1,0:T(8,128)} %shard_map.110.own), channel_id=1, source_target_pairs={{0,8},{2,26},{4,12},{6,30},{8,0},{10,18},{12,4},{14,22},{16,24},{1... | collective-permute-start | bytes 1572872 | tf_op jit(solution)/shard_map/ppermute | solution.py:155
  96.1 28.6 %collective-permute-start.17 = (f32[256,512]{1,0:T(8,128)}, f32[256,512]{1,0:T(8,128)}, u32[]{:S(2)}, u32[]{:S(2)}) collective-permute-start(f32[256,512]{1,0:T(8,128)} %shard_map.106.own), channel_id=1, source_target_pairs={{0,8},{2,26},{4,12},{6,30},{8,0},{10,18},{12,4},{14,22},{16,24},{1... | collective-permute-start | bytes 1572872 | tf_op jit(solution)/shard_map/ppermute | solution.py:155
  100.0 16.1 %collective-permute-start.9 = (f32[256,256]{1,0:T(8,128)S(1)}, f32[256,256]{1,0:T(8,128)S(1)}, u32[]{:S(2)}, u32[]{:S(2)}) collective-permute-start(f32[256,256]{1,0:T(8,128)S(1)} %collective-permute-done.7.a), channel_id=1, source_target_pairs={{0,24},{2,10},{4,28},{6,14},{8,16},{10,2},{12,20},{14,6},{16,8},{1... | collective-permute-start | bytes 786440 | tf_op jit(solution)/shard_map/ppermute | solution.py:155
  116.8 15.3 %collective-permute-start.28 = (f32[256,512]{1,0:T(8,128)}, f32[256,512]{1,0:T(8,128)}, u32[]{:S(2)}, u32[]{:S(2)}) collective-permute-start(f32[256,512]{1,0:T(8,128)} %shard_map.110.own), channel_id=1, source_target_pairs={{0,24},{2,10},{4,28},{6,14},{8,16},{10,2},{12,20},{14,6},{16,8},{1... | collective-permute-start | bytes 1572872 | tf_op jit(solution)/shard_map/ppermute | solution.py:155
  121.4 17.8 %collective-permute-start.39 = (f32[256,512]{1,0:T(8,128)}, f32[256,512]{1,0:T(8,128)}, u32[]{:S(2)}, u32[]{:S(2)}) collective-permute-start(f32[256,512]{1,0:T(8,128)} %collective-permute-done.37.a), channel_id=1, source_target_pairs={{0,24},{2,10},{4,28},{6,14},{8,16},{10,2},{12,20},{14,6},{16,8},{1... | collective-permute-start | bytes 1572872 | tf_op jit(solution)/shard_map/ppermute | solution.py:155
  124.6 20.2 %collective-permute-start.29 = (f32[256,512]{1,0:T(8,128)}, f32[256,512]{1,0:T(8,128)}, u32[]{:S(2)}, u32[]{:S(2)}) collective-permute-start(f32[256,512]{1,0:T(8,128)} %collective-permute-done.27.a), channel_id=1, source_target_pairs={{0,24},{2,10},{4,28},{6,14},{8,16},{10,2},{12,20},{14,6},{16,8},{1... | collective-permute-start | bytes 1572872 | tf_op jit(solution)/shard_map/ppermute | solution.py:155
  124.6 25.8 %collective-permute-start.19 = (f32[256,512]{1,0:T(8,128)}, f32[256,512]{1,0:T(8,128)}, u32[]{:S(2)}, u32[]{:S(2)}) collective-permute-start(f32[256,512]{1,0:T(8,128)} %collective-permute-done.17.a), channel_id=1, source_target_pairs={{0,24},{2,10},{4,28},{6,14},{8,16},{10,2},{12,20},{14,6},{16,8},{1... | collective-permute-start | bytes 1572872 | tf_op jit(solution)/shard_map/ppermute | solution.py:155
  132.1 20.9 %collective-permute-start.50 = (f32[256,256]{1,0:T(8,128)S(1)}, f32[256,256]{1,0:T(8,128)S(1)}, u32[]{:S(2)}, u32[]{:S(2)}) collective-permute-start(f32[256,256]{1,0:T(8,128)S(1)} %shard_map.119.own), channel_id=1, source_target_pairs={{0,32},{2,98},{4,36},{6,102},{8,40},{10,106},{12,44},{14,110},{16,... | collective-permute-start | bytes 786440 | tf_op jit(solution)/shard_map/ppermute | solution.py:155
  133.6 20.7 %collective-permute-start.51 = (f32[256,256]{1,0:T(8,128)S(1)}, f32[256,256]{1,0:T(8,128)S(1)}, u32[]{:S(2)}, u32[]{:S(2)}) collective-permute-start(f32[256,256]{1,0:T(8,128)S(1)} %shard_map.119.own), channel_id=1, source_target_pairs={{0,96},{2,34},{4,100},{6,38},{8,104},{10,42},{12,108},{14,46},{16,... | collective-permute-start | bytes 786440 | tf_op jit(solution)/shard_map/ppermute | solution.py:155
  139.2 17.7 %collective-permute-start.10 = (f32[256,256]{1,0:T(8,128)S(1)}, f32[256,256]{1,0:T(8,128)S(1)}, u32[]{:S(2)}, u32[]{:S(2)}) collective-permute-start(f32[256,256]{1,0:T(8,128)S(1)} %shard_map.102.own), channel_id=1, source_target_pairs={{0,32},{2,98},{4,36},{6,102},{8,40},{10,106},{12,44},{14,110},{16,... | collective-permute-start | bytes 786440 | tf_op jit(solution)/shard_map/ppermute | solution.py:155
  144.8 27.3 %collective-permute-start.40 = (f32[256,512]{1,0:T(8,128)S(1)}, f32[256,512]{1,0:T(8,128)S(1)}, u32[]{:S(2)}, u32[]{:S(2)}) collective-permute-start(f32[256,512]{1,0:T(8,128)S(1)} %shard_map.115.own), channel_id=1, source_target_pairs={{0,32},{2,98},{4,36},{6,102},{8,40},{10,106},{12,44},{14,110},{16,... | collective-permute-start | bytes 1572872 | tf_op jit(solution)/shard_map/ppermute | solution.py:155
  150.5 22.1 %collective-permute-start.30 = (f32[256,512]{1,0:T(8,128)S(1)}, f32[256,512]{1,0:T(8,128)S(1)}, u32[]{:S(2)}, u32[]{:S(2)}) collective-permute-start(f32[256,512]{1,0:T(8,128)S(1)} %shard_map.111.own), channel_id=1, source_target_pairs={{0,32},{2,98},{4,36},{6,102},{8,40},{10,106},{12,44},{14,110},{16,... | collective-permute-start | bytes 1572872 | tf_op jit(solution)/shard_map/ppermute | solution.py:155
  153.1 21.1 %collective-permute-start.41 = (f32[256,512]{1,0:T(8,128)S(1)}, f32[256,512]{1,0:T(8,128)S(1)}, u32[]{:S(2)}, u32[]{:S(2)}) collective-permute-start(f32[256,512]{1,0:T(8,128)S(1)} %shard_map.115.own), channel_id=1, source_target_pairs={{0,96},{2,34},{4,100},{6,38},{8,104},{10,42},{12,108},{14,46},{16,... | collective-permute-start | bytes 1572872 | tf_op jit(solution)/shard_map/ppermute | solution.py:155
  154.3 20.3 %collective-permute-start.20 = (f32[256,512]{1,0:T(8,128)S(1)}, f32[256,512]{1,0:T(8,128)S(1)}, u32[]{:S(2)}, u32[]{:S(2)}) collective-permute-start(f32[256,512]{1,0:T(8,128)S(1)} %shard_map.107.own), channel_id=1, source_target_pairs={{0,32},{2,98},{4,36},{6,102},{8,40},{10,106},{12,44},{14,110},{16,... | collective-permute-start | bytes 1572872 | tf_op jit(solution)/shard_map/ppermute | solution.py:155
  156.9 13.6 %collective-permute-start.52 = (f32[256,256]{1,0:T(8,128)S(1)}, f32[256,256]{1,0:T(8,128)S(1)}, u32[]{:S(2)}, u32[]{:S(2)}) collective-permute-start(f32[256,256]{1,0:T(8,128)S(1)} %collective-permute-done.50.a), channel_id=1, source_target_pairs={{0,96},{2,34},{4,100},{6,38},{8,104},{10,42},{12,108},{14,46},{16,... | collective-permute-start | bytes 786440 | tf_op jit(solution)/shard_map/ppermute | solution.py:155
  172.6 20.8 %collective-permute-start.32 = (f32[256,512]{1,0:T(8,128)S(1)}, f32[256,512]{1,0:T(8,128)S(1)}, u32[]{:S(2)}, u32[]{:S(2)}) collective-permute-start(f32[256,512]{1,0:T(8,128)S(1)} %collective-permute-done.30.a), channel_id=1, source_target_pairs={{0,96},{2,34},{4,100},{6,38},{8,104},{10,42},{12,108},{14,46},{16,... | collective-permute-start | bytes 1572872 | tf_op jit(solution)/shard_map/ppermute | solution.py:155
  174.2 22.4 %collective-permute-start.21 = (f32[256,512]{1,0:T(8,128)S(1)}, f32[256,512]{1,0:T(8,128)S(1)}, u32[]{:S(2)}, u32[]{:S(2)}) collective-permute-start(f32[256,512]{1,0:T(8,128)S(1)} %shard_map.107.own), channel_id=1, source_target_pairs={{0,96},{2,34},{4,100},{6,38},{8,104},{10,42},{12,108},{14,46},{16,... | collective-permute-start | bytes 1572872 | tf_op jit(solution)/shard_map/ppermute | solution.py:155
  174.6 27.6 %collective-permute-start.22 = (f32[256,512]{1,0:T(8,128)S(1)}, f32[256,512]{1,0:T(8,128)S(1)}, u32[]{:S(2)}, u32[]{:S(2)}) collective-permute-start(f32[256,512]{1,0:T(8,128)S(1)} %collective-permute-done.20.a), channel_id=1, source_target_pairs={{0,96},{2,34},{4,100},{6,38},{8,104},{10,42},{12,108},{14,46},{16,... | collective-permute-start | bytes 1572872 | tf_op jit(solution)/shard_map/ppermute | solution.py:155
  182.2 22.8 %collective-permute-start.11 = (f32[256,256]{1,0:T(8,128)S(1)}, f32[256,256]{1,0:T(8,128)S(1)}, u32[]{:S(2)}, u32[]{:S(2)}) collective-permute-start(f32[256,256]{1,0:T(8,128)S(1)} %shard_map.102.own), channel_id=1, source_target_pairs={{0,96},{2,34},{4,100},{6,38},{8,104},{10,42},{12,108},{14,46},{16,... | collective-permute-start | bytes 786440 | tf_op jit(solution)/shard_map/ppermute | solution.py:155
  185.3 22.5 %collective-permute-start.12 = (f32[256,256]{1,0:T(8,128)S(1)}, f32[256,256]{1,0:T(8,128)S(1)}, u32[]{:S(2)}, u32[]{:S(2)}) collective-permute-start(f32[256,256]{1,0:T(8,128)S(1)} %collective-permute-done.10.a), channel_id=1, source_target_pairs={{0,96},{2,34},{4,100},{6,38},{8,104},{10,42},{12,108},{14,46},{16,... | collective-permute-start | bytes 786440 | tf_op jit(solution)/shard_map/ppermute | solution.py:155
  (97 other events, 1146.5 us)

commit v2 on v1

--- a/solution.py
+++ b/solution.py
@@ -9,8 +9,9 @@
 
 
 F32, BF16 = jnp.float32, jnp.bfloat16
-WIDTHS = (256, 512, 512, 512, 256)
-STARTS = (0, 512, 1024, 1536, 256)
+WIDTHS = (256, 512, 512, 384, 384)
+STARTS = (768, 1024, 1536, 0, 384)
+SPLIT = (1, 2)
 
 
 def mm(a, b):
@@ -131,9 +132,11 @@
         out[rows, :] = product(w[p], x)
 
 
-def near_kernel(start, place, w, own, one, three, halo, cross, right, out):
+def near_kernel(start, place, w, own, one, three, halo, *refs):
+    right, out = refs[-2:]
     here = slice(start, start + out.shape[1])
-    third = jnp.where(place[2] == 1, halo[...] + cross[...], three[...])
+    edge = halo[...] + refs[0][...] if len(refs) == 3 else halo[...]
+    third = jnp.where(place[2] == 1, edge, three[...])
     x = jnp.concatenate([own[...], one[:, here], third], axis=0)
     out[...] = right[:, here] - product(w[...], x)
 
@@ -155,11 +158,15 @@
     return lax.ppermute(x, "row", [(i, i ^ (odd_bits if i % 2 else bits)) for i in range(count)])
 
 
-def halo_of(two, crossing):
+def halo_of(k, two, three, part):
     count = lax.axis_size("row")
-    route = [(i, i + 3) for i in range(1, count - 3, 4)]
-    route = [(i, j) for i, j in route if (i // 16 != j // 16) == crossing]
-    return lax.ppermute(two, "row", route + [(j + 2, i + 2) for i, j in route])
+    ends = [(i, i + 1) for i in range(3, count - 1, 4)]
+    if part is not None:
+        ends = [(i, j) for i, j in ends if (i // 16 != j // 16) == part]
+    odd = k % 2
+    route = [((i ^ 3) if odd else (i ^ 2), j) for i, j in ends]
+    route += [((j ^ 3) if odd else (j ^ 2), i) for i, j in ends]
+    return lax.ppermute(three if odd else two, "row", route)
 
 
 VM = pl.BlockSpec(memory_space=pltpu.VMEM)
@@ -235,13 +242,13 @@
         flops = 2 * 3 * 2 * 4 * b * b * w
         piece = shape((rows, w), F32)
         three = xor(two[k], 1)
-        halo = halo_of(two[k], False)
-        cross = halo_of(two[k], True)
+        halo = halo_of(k, two[k], three, False if k in SPLIT else None)
+        cross = halo_of(k, two[k], three, True) if k in SPLIT else None
         coeffs = call(functools.partial(stage_x_kernel, s), [VM] * 5, piece, flops, wx, raw[k], one, two[k], three)
         coeffs = call(stage_z_kernel, [VM] * 5, piece, flops, wz, *gathered(coeffs, 4, 12))
         part = call(
-            functools.partial(near_kernel, s), [SM] + [VM] * 7, piece, 2 * flops,
-            place, wn, raw[k], one, three, halo, cross, right_side,
+            functools.partial(near_kernel, s), [SM] + [VM] * (7 if k in SPLIT else 6), piece, 2 * flops,
+            *([place, wn, raw[k], one, three, halo] + ([cross] if k in SPLIT else []) + [right_side]),
         )
         ins = gathered(coeffs, 16, 48)
         olds = () if result is None else (result,)

time: 218 us -> 215 us (0.986)
  starting transfers between devices: 75.7 us -> 73.3 us
    ppermute x10 -> x7, waiting for transfers between devices: 5.03 us -> 10.9 us  [halo_of(): return lax.ppermute(three if odd else two, 'row', route)]
    ppermute x44, waiting for transfers between devices: 84.8 us -> 79.7 us  [xor(): lax.ppermute(x, 'row', [(i, i ^ (odd_bits if i % 2 else bits)) for i in r...]
    ppermute x10 -> x7, starting transfers between devices: 16.6 us -> 14 us  [halo_of(): return lax.ppermute(three if odd else two, 'row', route)]
    unnamed x146 -> x130, local copies, waits for them, and re-layouts: 13.1 us -> 11 us
  transfers between devices with their start and end apart: 56 -> 53, of which waited for: 24 -> 21; matrix products, arithmetic and copies ran while one was open for 0% -> 0% of each run, Pallas kernels for 13% -> 14%
where the time goes in v2:
time: 215 us; the launch traced here: 213 us
  waiting for transfers between devices  96.2 us (45%)
  starting transfers between devices  73.3 us (34%)
  Pallas kernels  30.7 us (14%)
  local copies, waits for them, and re-layouts  11 us (5%)
    ppermute x44, waiting for transfers between devices, xor(): lax.ppermute(x, 'row', [(i, i ^ (odd_bits if i % 2 else bits)) for i in r...  79.7 us
    ppermute x44, starting transfers between devices, xor(): lax.ppermute(x, 'row', [(i, i ^ (odd_bits if i % 2 else bits)) for i in r...  57.4 us
    pallas_call x31, Pallas kernels, call(): pl.pallas_call(kernel, in_specs=in_specs, out_shape=out_shape, cost_estim...  30.7 us
    ppermute x7, starting transfers between devices, halo_of(): return lax.ppermute(three if odd else two, 'row', route)  14 us
    unnamed x130, local copies, waits for them, and re-layouts  11 us
    ppermute x7, waiting for transfers between devices, halo_of(): return lax.ppermute(three if odd else two, 'row', route)  10.9 us
  transfers between devices with their start and end apart: 53, of which 21 were waited for; matrix products, arithmetic and copies ran while one was open for 0% of the time, Pallas kernels for 14%

profile of v2, /device:TPU:14, one launch (start us, length us, event | category | flops | bytes accessed | tf_op | source)
XLA Modules:
  0.0 213.5 jit_solution(13738008716201957425)
XLA Ops:
  3.2 4.0 %collective-permute-start.1 = (f32[2,2,128,128]{3,2,1,0:T(8,128)S(1)}, f32[2,2,128,128]{3,2,1,0:T(8,128)S(1)}, u32[]{:S(2)}, u32[]{:S(2)}) collective-permute-start(f32[2,2,128,128]{3,2,1,0:T(8,128)S(1)} %get-tuple-element.15), channel_id=1, source_target_pairs={{0,16},{2,18},{4,20},{6,22},{8,24},{10,26},{12,28},{14,30},{16,0},... | collective-permute-start | bytes 786440 | tf_op jit(solution)/shard_map/ppermute | solution.py:158
  9.4 2.3 %collective-permute-start = (f32[2,2,128,128]{3,2,1,0:T(8,128)S(1)}, f32[2,2,128,128]{3,2,1,0:T(8,128)S(1)}, u32[]{:S(2)}, u32[]{:S(2)}) collective-permute-start(f32[2,2,128,128]{3,2,1,0:T(8,128)S(1)} %get-tuple-element.14), channel_id=1, source_target_pairs={{0,64},{2,66},{4,68},{6,70},{8,72},{10,74},{12,76},{14,78},{16,80}... | collective-permute-start | bytes 786440 | tf_op jit(solution)/shard_map/ppermute | solution.py:158
  17.3 2.0 collective-permute-done.o4
  25.7 7.6 %collective-permute-done.5.two = f32[256,384]{1,0:T(8,128)S(1)} collective-permute-done((f32[256,384]{1,0:T(8,128)S(1)}, f32[256,384]{1,0:T(8,128)S(1)}, u32[]{:S(2)}, u32[]{:S(2)}) %collective-permute-start.5) | collective-permute-done | bytes 393248 | tf_op jit(solution)/shard_map/ppermute | solution.py:158
  33.3 2.6 %collective-permute-start.51 = (f32[256,256]{1,0:T(8,128)S(1)}, f32[256,256]{1,0:T(8,128)S(1)}, u32[]{:S(2)}, u32[]{:S(2)}) collective-permute-start(f32[256,256]{1,0:T(8,128)S(1)} %collective-permute-done.43.two), channel_id=1, source_target_pairs={{2,8},{10,16},{18,24},{26,32},{34,40},{42,48},{50,56},{58,64},{66,... | collective-permute-start | bytes 786440 | tf_op jit(solution)/shard_map/ppermute | solution.py:169
  35.9 8.6 %collective-permute-done.33.two = f32[256,512]{1,0:T(8,128)S(1)} collective-permute-done((f32[256,512]{1,0:T(8,128)S(1)}, f32[256,512]{1,0:T(8,128)S(1)}, u32[]{:S(2)}, u32[]{:S(2)}) %collective-permute-start.33) | collective-permute-done | bytes 524320 | tf_op jit(solution)/shard_map/ppermute | solution.py:158
  45.7 9.1 %collective-permute-done.23.two = f32[256,512]{1,0:T(8,128)S(1)} collective-permute-done((f32[256,512]{1,0:T(8,128)S(1)}, f32[256,512]{1,0:T(8,128)S(1)}, u32[]{:S(2)}, u32[]{:S(2)}) %collective-permute-start.23) | collective-permute-done | bytes 524320 | tf_op jit(solution)/shard_map/ppermute | solution.py:158
  54.9 2.6 %collective-permute-start.13 = (f32[256,384]{1,0:T(8,128)S(1)}, f32[256,384]{1,0:T(8,128)S(1)}, u32[]{:S(2)}, u32[]{:S(2)}) collective-permute-start(f32[256,384]{1,0:T(8,128)S(1)} %collective-permute-done.5.two), channel_id=1, source_target_pairs={{2,8},{10,16},{18,24},{26,32},{34,40},{42,48},{50,56},{58,64},{66,... | collective-permute-start | bytes 1179656 | tf_op jit(solution)/shard_map/ppermute | solution.py:169
  58.2 4.5 %collective-permute-done.13.halo = f32[256,384]{1,0:T(8,128)S(1)} collective-permute-done((f32[256,384]{1,0:T(8,128)S(1)}, f32[256,384]{1,0:T(8,128)S(1)}, u32[]{:S(2)}, u32[]{:S(2)}) %collective-permute-start.13) | collective-permute-done | bytes 393248 | tf_op jit(solution)/shard_map/ppermute | solution.py:169
  63.5 5.9 %collective-permute-start.32 = (f32[256,512]{1,0:T(8,128)S(1)}, f32[256,512]{1,0:T(8,128)S(1)}, u32[]{:S(2)}, u32[]{:S(2)}) collective-permute-start(f32[256,512]{1,0:T(8,128)S(1)} %collective-permute-done.23.two), channel_id=1, source_target_pairs={{26,32},{58,64},{90,96},{36,30},{68,62},{100,94},{27,33},{59,65},{... | collective-permute-start | bytes 1572872 | tf_op jit(solution)/shard_map/ppermute | solution.py:169
  73.3 6.3 %collective-permute-done.32.refs_0_ = f32[256,512]{1,0:T(8,128)S(1)} collective-permute-done((f32[256,512]{1,0:T(8,128)S(1)}, f32[256,512]{1,0:T(8,128)S(1)}, u32[]{:S(2)}, u32[]{:S(2)}) %collective-permute-start.32) | collective-permute-done | bytes 524320 | tf_op jit(solution)/shard_map/ppermute | solution.py:169
  83.2 3.3 %collective-permute-start.17 = (f32[256,384]{1,0:T(8,128)S(1)}, f32[256,384]{1,0:T(8,128)S(1)}, u32[]{:S(2)}, u32[]{:S(2)}) collective-permute-start(f32[256,384]{1,0:T(8,128)S(1)} %shard_map.106.own), channel_id=1, source_target_pairs={{0,24},{2,10},{4,28},{6,14},{8,16},{10,2},{12,20},{14,6},{16,8},{1... | collective-permute-start | bytes 1179656 | tf_op jit(solution)/shard_map/ppermute | solution.py:158
  89.4 3.3 %collective-permute-done.46.b = f32[256,256]{1,0:T(8,128)S(1)} collective-permute-done((f32[256,256]{1,0:T(8,128)S(1)}, f32[256,256]{1,0:T(8,128)S(1)}, u32[]{:S(2)}, u32[]{:S(2)}) %collective-permute-start.46) | collective-permute-done | bytes 262176 | tf_op jit(solution)/shard_map/ppermute | solution.py:158
  93.4 3.7 %collective-permute-start.36 = (f32[256,512]{1,0:T(8,128)S(1)}, f32[256,512]{1,0:T(8,128)S(1)}, u32[]{:S(2)}, u32[]{:S(2)}) collective-permute-start(f32[256,512]{1,0:T(8,128)S(1)} %shard_map.114.own), channel_id=1, source_target_pairs={{0,24},{2,10},{4,28},{6,14},{8,16},{10,2},{12,20},{14,6},{16,8},{1... | collective-permute-start | bytes 1572872 | tf_op jit(solution)/shard_map/ppermute | solution.py:158
  97.1 4.0 %collective-permute-done.17.b = f32[256,384]{1,0:T(8,128)S(1)} collective-permute-done((f32[256,384]{1,0:T(8,128)S(1)}, f32[256,384]{1,0:T(8,128)S(1)}, u32[]{:S(2)}, u32[]{:S(2)}) %collective-permute-start.17) | collective-permute-done | bytes 393248 | tf_op jit(solution)/shard_map/ppermute | solution.py:158
  101.9 3.7 %collective-permute-start.47 = (f32[256,256]{1,0:T(8,128)S(1)}, f32[256,256]{1,0:T(8,128)S(1)}, u32[]{:S(2)}, u32[]{:S(2)}) collective-permute-start(f32[256,256]{1,0:T(8,128)S(1)} %collective-permute-done.45.a), channel_id=1, source_target_pairs={{0,24},{2,10},{4,28},{6,14},{8,16},{10,2},{12,20},{14,6},{16,8},{1... | collective-permute-start | bytes 786440 | tf_op jit(solution)/shard_map/ppermute | solution.py:158
  105.6 3.2 %collective-permute-start.26 = (f32[256,512]{1,0:T(8,128)}, f32[256,512]{1,0:T(8,128)}, u32[]{:S(2)}, u32[]{:S(2)}) collective-permute-start(f32[256,512]{1,0:T(8,128)} %shard_map.110.own), channel_id=1, source_target_pairs={{0,24},{2,10},{4,28},{6,14},{8,16},{10,2},{12,20},{14,6},{16,8},{1... | collective-permute-start | bytes 1572872 | tf_op jit(solution)/shard_map/ppermute | solution.py:158
  108.8 9.1 %collective-permute-done.47.c = f32[256,256]{1,0:T(8,128)S(1)} collective-permute-done((f32[256,256]{1,0:T(8,128)S(1)}, f32[256,256]{1,0:T(8,128)S(1)}, u32[]{:S(2)}, u32[]{:S(2)}) %collective-permute-start.47) | collective-permute-done | bytes 262176 | tf_op jit(solution)/shard_map/ppermute | solution.py:158
  118.7 3.7 %collective-permute-start.8 = (f32[256,384]{1,0:T(8,128)}, f32[256,384]{1,0:T(8,128)}, u32[]{:S(2)}, u32[]{:S(2)}) collective-permute-start(f32[256,384]{1,0:T(8,128)} %shard_map.101.own), channel_id=1, source_target_pairs={{0,24},{2,10},{4,28},{6,14},{8,16},{10,2},{12,20},{14,6},{16,8},{1... | collective-permute-start | bytes 1179656 | tf_op jit(solution)/shard_map/ppermute | solution.py:158
  123.2 3.2 %collective-permute-start.27 = (f32[256,512]{1,0:T(8,128)}, f32[256,512]{1,0:T(8,128)}, u32[]{:S(2)}, u32[]{:S(2)}) collective-permute-start(f32[256,512]{1,0:T(8,128)} %collective-permute-done.25.a), channel_id=1, source_target_pairs={{0,24},{2,10},{4,28},{6,14},{8,16},{10,2},{12,20},{14,6},{16,8},{1... | collective-permute-start | bytes 1572872 | tf_op jit(solution)/shard_map/ppermute | solution.py:158
  132.7 7.7 %collective-permute-done.8.b = f32[256,384]{1,0:T(8,128)} collective-permute-done((f32[256,384]{1,0:T(8,128)}, f32[256,384]{1,0:T(8,128)}, u32[]{:S(2)}, u32[]{:S(2)}) %collective-permute-start.8) | collective-permute-done | bytes 393248 | tf_op jit(solution)/shard_map/ppermute | solution.py:158
  142.0 2.6 %collective-permute-done.18.c = f32[256,384]{1,0:T(8,128)} collective-permute-done((f32[256,384]{1,0:T(8,128)}, f32[256,384]{1,0:T(8,128)}, u32[]{:S(2)}, u32[]{:S(2)}) %collective-permute-start.18) | collective-permute-done | bytes 393248 | tf_op jit(solution)/shard_map/ppermute | solution.py:158
  144.7 3.7 %collective-permute-start.9 = (f32[256,384]{1,0:T(8,128)S(1)}, f32[256,384]{1,0:T(8,128)S(1)}, u32[]{:S(2)}, u32[]{:S(2)}) collective-permute-start(f32[256,384]{1,0:T(8,128)S(1)} %copy-done.43), channel_id=1, source_target_pairs={{0,24},{2,10},{4,28},{6,14},{8,16},{10,2},{12,20},{14,6},{16,8},{1... | collective-permute-start | bytes 1179656 | tf_op jit(solution)/shard_map/ppermute | solution.py:158
  151.9 2.1 %shard_map.111.own = f32[256,512]{1,0:T(8,128)S(1)} custom-call(bf16[2,256,512]{2,1,0:T(8,128)(2,1)S(1)} %shard_map.97.w, f32[256,512]{1,0:T(8,128)} %shard_map.110.own, f32[256,512]{1,0:T(8,128)} %collective-permute-done.25.a, f32[256,512]{1,0:T(8,128)} %collective-permute-done.26.b, f32[256,512]{1,0:T(8,128)} %collective-permute-done.27.c), custom_call_target="tpu_custom_call" | custom-call | flops 402653184 | bytes 655360 | tf_op jit(solution)/shard_map/pallas_call | solution.py:180
  154.1 2.6 %collective-permute-start.28 = (f32[256,512]{1,0:T(8,128)S(1)}, f32[256,512]{1,0:T(8,128)S(1)}, u32[]{:S(2)}, u32[]{:S(2)}) collective-permute-start(f32[256,512]{1,0:T(8,128)S(1)} %shard_map.111.own), channel_id=1, source_target_pairs={{0,32},{2,98},{4,36},{6,102},{8,40},{10,106},{12,44},{14,110},{16,... | collective-permute-start | bytes 1572872 | tf_op jit(solution)/shard_map/ppermute | solution.py:158
  157.1 2.7 %collective-permute-done.50.c = f32[256,256]{1,0:T(8,128)S(1)} collective-permute-done((f32[256,256]{1,0:T(8,128)S(1)}, f32[256,256]{1,0:T(8,128)S(1)}, u32[]{:S(2)}, u32[]{:S(2)}) %collective-permute-start.50) | collective-permute-done | bytes 262176 | tf_op jit(solution)/shard_map/ppermute | solution.py:158
  163.6 4.1 %collective-permute-start.10 = (f32[256,384]{1,0:T(8,128)S(1)}, f32[256,384]{1,0:T(8,128)S(1)}, u32[]{:S(2)}, u32[]{:S(2)}) collective-permute-start(f32[256,384]{1,0:T(8,128)S(1)} %shard_map.102.own), channel_id=1, source_target_pairs={{0,32},{2,98},{4,36},{6,102},{8,40},{10,106},{12,44},{14,110},{16,... | collective-permute-start | bytes 1179656 | tf_op jit(solution)/shard_map/ppermute | solution.py:158
  167.7 5.7 %collective-permute-done.28.a = f32[256,512]{1,0:T(8,128)S(1)} collective-permute-done((f32[256,512]{1,0:T(8,128)S(1)}, f32[256,512]{1,0:T(8,128)S(1)}, u32[]{:S(2)}, u32[]{:S(2)}) %collective-permute-start.28) | collective-permute-done | bytes 524320 | tf_op jit(solution)/shard_map/ppermute | solution.py:158
  178.2 3.6 %collective-permute-done.10.a = f32[256,384]{1,0:T(8,128)S(1)} collective-permute-done((f32[256,384]{1,0:T(8,128)S(1)}, f32[256,384]{1,0:T(8,128)S(1)}, u32[]{:S(2)}, u32[]{:S(2)}) %collective-permute-start.10) | collective-permute-done | bytes 393248 | tf_op jit(solution)/shard_map/ppermute | solution.py:158
  196.8 5.4 %collective-permute-done.21.c = f32[256,384]{1,0:T(8,128)S(1)} collective-permute-done((f32[256,384]{1,0:T(8,128)S(1)}, f32[256,384]{1,0:T(8,128)S(1)}, u32[]{:S(2)}, u32[]{:S(2)}) %collective-permute-start.21) | collective-permute-done | bytes 393248 | tf_op jit(solution)/shard_map/ppermute | solution.py:158
  203.5 2.9 %collective-permute-done.12.c = f32[256,384]{1,0:T(8,128)S(1)} collective-permute-done((f32[256,384]{1,0:T(8,128)S(1)}, f32[256,384]{1,0:T(8,128)S(1)}, u32[]{:S(2)}, u32[]{:S(2)}) %collective-permute-start.12) | collective-permute-done | bytes 393248 | tf_op jit(solution)/shard_map/ppermute | solution.py:158
  209.1 3.7 %collective-permute-done.52 = f32[2,128]{1,0:T(2,128)S(1)} collective-permute-done((f32[2,128]{1,0:T(2,128)S(1)}, f32[2,128]{1,0:T(2,128)S(1)}, u32[]{:S(2)}, u32[]{:S(2)}) %collective-permute-start.52) | collective-permute-done | bytes 1056 | tf_op jit(solution)/shard_map/ppermute | solution.py:264
  (238 shorter events, 72.1 us)
Async XLA Ops:
  0.6 70.3 %collective-permute-start.4 = (f32[256,2048]{1,0:T(8,128)}, f32[256,2048]{1,0:T(8,128)S(1)}, u32[]{:S(2)}, u32[]{:S(2)}) collective-permute-start(f32[256,2048]{1,0:T(8,128)} %x.17), channel_id=1, source_target_pairs={{0,2},{2,0},{4,6},{6,4},{8,10},{10,8},{12,14},{14,12},{16,18},{18,... | collective-permute-start | bytes 6291464 | tf_op jit(solution)/shard_map/ppermute | solution.py:158
  8.1 16.7 %collective-permute-start.14 = (f32[256,384]{1,0:T(8,128)S(1)}, f32[256,384]{1,0:T(8,128)S(1)}, u32[]{:S(2)}, u32[]{:S(2)}) collective-permute-start(f32[256,384]{1,0:T(8,128)S(1)} %shard_map.105.own), channel_id=1, source_target_pairs={{0,4},{2,6},{4,0},{6,2},{8,12},{10,14},{12,8},{14,10},{16,20},{18,... | collective-permute-start | bytes 1179656 | tf_op jit(solution)/shard_map/ppermute | solution.py:158
  16.4 16.9 %collective-permute-start.5 = (f32[256,384]{1,0:T(8,128)S(1)}, f32[256,384]{1,0:T(8,128)S(1)}, u32[]{:S(2)}, u32[]{:S(2)}) collective-permute-start(f32[256,384]{1,0:T(8,128)S(1)} %shard_map.100.own), channel_id=1, source_target_pairs={{0,4},{2,6},{4,0},{6,2},{8,12},{10,14},{12,8},{14,10},{16,20},{18,... | collective-permute-start | bytes 1179656 | tf_op jit(solution)/shard_map/ppermute | solution.py:158
  20.1 24.5 %collective-permute-start.33 = (f32[256,512]{1,0:T(8,128)S(1)}, f32[256,512]{1,0:T(8,128)S(1)}, u32[]{:S(2)}, u32[]{:S(2)}) collective-permute-start(f32[256,512]{1,0:T(8,128)S(1)} %shard_map.113.own), channel_id=1, source_target_pairs={{0,4},{2,6},{4,0},{6,2},{8,12},{10,14},{12,8},{14,10},{16,20},{18,... | collective-permute-start | bytes 1572872 | tf_op jit(solution)/shard_map/ppermute | solution.py:158
  24.8 30.0 %collective-permute-start.23 = (f32[256,512]{1,0:T(8,128)S(1)}, f32[256,512]{1,0:T(8,128)S(1)}, u32[]{:S(2)}, u32[]{:S(2)}) collective-permute-start(f32[256,512]{1,0:T(8,128)S(1)} %shard_map.109.own), channel_id=1, source_target_pairs={{0,4},{2,6},{4,0},{6,2},{8,12},{10,14},{12,8},{14,10},{16,20},{18,... | collective-permute-start | bytes 1572872 | tf_op jit(solution)/shard_map/ppermute | solution.py:158
  33.3 21.6 %collective-permute-start.15 = (f32[256,384]{1,0:T(8,128)S(1)}, f32[256,384]{1,0:T(8,128)S(1)}, u32[]{:S(2)}, u32[]{:S(2)}) collective-permute-start(f32[256,384]{1,0:T(8,128)S(1)} %collective-permute-done.14.two), channel_id=1, source_target_pairs={{0,2},{2,0},{4,6},{6,4},{8,10},{10,8},{12,14},{14,12},{16,18},{18,... | collective-permute-start | bytes 1179656 | tf_op jit(solution)/shard_map/ppermute | solution.py:158
  44.5 25.0 %collective-permute-start.34 = (f32[256,512]{1,0:T(8,128)S(1)}, f32[256,512]{1,0:T(8,128)S(1)}, u32[]{:S(2)}, u32[]{:S(2)}) collective-permute-start(f32[256,512]{1,0:T(8,128)S(1)} %collective-permute-done.33.two), channel_id=1, source_target_pairs={{0,2},{2,0},{4,6},{6,4},{8,10},{10,8},{12,14},{14,12},{16,18},{18,... | collective-permute-start | bytes 1572872 | tf_op jit(solution)/shard_map/ppermute | solution.py:158
  54.9 15.3 %collective-permute-start.24 = (f32[256,512]{1,0:T(8,128)S(1)}, f32[256,512]{1,0:T(8,128)S(1)}, u32[]{:S(2)}, u32[]{:S(2)}) collective-permute-start(f32[256,512]{1,0:T(8,128)S(1)} %collective-permute-done.23.two), channel_id=1, source_target_pairs={{0,2},{2,0},{4,6},{6,4},{8,10},{10,8},{12,14},{14,12},{16,18},{18,... | collective-permute-start | bytes 1572872 | tf_op jit(solution)/shard_map/ppermute | solution.py:158
  63.5 16.2 %collective-permute-start.32 = (f32[256,512]{1,0:T(8,128)S(1)}, f32[256,512]{1,0:T(8,128)S(1)}, u32[]{:S(2)}, u32[]{:S(2)}) collective-permute-start(f32[256,512]{1,0:T(8,128)S(1)} %collective-permute-done.23.two), channel_id=1, source_target_pairs={{26,32},{58,64},{90,96},{36,30},{68,62},{100,94},{27,33},{59,65},{... | collective-permute-start | bytes 1572872 | tf_op jit(solution)/shard_map/ppermute | solution.py:169
  72.8 24.2 %collective-permute-start.16 = (f32[256,384]{1,0:T(8,128)S(1)}, f32[256,384]{1,0:T(8,128)}, u32[]{:S(2)}, u32[]{:S(2)}) collective-permute-start(f32[256,384]{1,0:T(8,128)S(1)} %shard_map.106.own), channel_id=1, source_target_pairs={{0,8},{2,26},{4,12},{6,30},{8,0},{10,18},{12,4},{14,22},{16,24},{1... | collective-permute-start | bytes 1179656 | tf_op jit(solution)/shard_map/ppermute | solution.py:158
  81.2 24.3 %collective-permute-start.35 = (f32[256,512]{1,0:T(8,128)S(1)}, f32[256,512]{1,0:T(8,128)}, u32[]{:S(2)}, u32[]{:S(2)}) collective-permute-start(f32[256,512]{1,0:T(8,128)S(1)} %shard_map.114.own), channel_id=1, source_target_pairs={{0,8},{2,26},{4,12},{6,30},{8,0},{10,18},{12,4},{14,22},{16,24},{1... | collective-permute-start | bytes 1572872 | tf_op jit(solution)/shard_map/ppermute | solution.py:158
  83.2 17.9 %collective-permute-start.17 = (f32[256,384]{1,0:T(8,128)S(1)}, f32[256,384]{1,0:T(8,128)S(1)}, u32[]{:S(2)}, u32[]{:S(2)}) collective-permute-start(f32[256,384]{1,0:T(8,128)S(1)} %shard_map.106.own), channel_id=1, source_target_pairs={{0,24},{2,10},{4,28},{6,14},{8,16},{10,2},{12,20},{14,6},{16,8},{1... | collective-permute-start | bytes 1179656 | tf_op jit(solution)/shard_map/ppermute | solution.py:158
  87.9 17.7 %collective-permute-start.7 = (f32[256,384]{1,0:T(8,128)}, f32[256,384]{1,0:T(8,128)S(1)}, u32[]{:S(2)}, u32[]{:S(2)}) collective-permute-start(f32[256,384]{1,0:T(8,128)} %shard_map.101.own), channel_id=1, source_target_pairs={{0,8},{2,26},{4,12},{6,30},{8,0},{10,18},{12,4},{14,22},{16,24},{1... | collective-permute-start | bytes 1179656 | tf_op jit(solution)/shard_map/ppermute | solution.py:158
  93.4 29.0 %collective-permute-start.36 = (f32[256,512]{1,0:T(8,128)S(1)}, f32[256,512]{1,0:T(8,128)S(1)}, u32[]{:S(2)}, u32[]{:S(2)}) collective-permute-start(f32[256,512]{1,0:T(8,128)S(1)} %shard_map.114.own), channel_id=1, source_target_pairs={{0,24},{2,10},{4,28},{6,14},{8,16},{10,2},{12,20},{14,6},{16,8},{1... | collective-permute-start | bytes 1572872 | tf_op jit(solution)/shard_map/ppermute | solution.py:158
  97.1 26.2 %collective-permute-start.25 = (f32[256,512]{1,0:T(8,128)}, f32[256,512]{1,0:T(8,128)}, u32[]{:S(2)}, u32[]{:S(2)}) collective-permute-start(f32[256,512]{1,0:T(8,128)} %shard_map.110.own), channel_id=1, source_target_pairs={{0,8},{2,26},{4,12},{6,30},{8,0},{10,18},{12,4},{14,22},{16,24},{1... | collective-permute-start | bytes 1572872 | tf_op jit(solution)/shard_map/ppermute | solution.py:158
  101.9 16.1 %collective-permute-start.47 = (f32[256,256]{1,0:T(8,128)S(1)}, f32[256,256]{1,0:T(8,128)S(1)}, u32[]{:S(2)}, u32[]{:S(2)}) collective-permute-start(f32[256,256]{1,0:T(8,128)S(1)} %collective-permute-done.45.a), channel_id=1, source_target_pairs={{0,24},{2,10},{4,28},{6,14},{8,16},{10,2},{12,20},{14,6},{16,8},{1... | collective-permute-start | bytes 786440 | tf_op jit(solution)/shard_map/ppermute | solution.py:158
  105.6 24.8 %collective-permute-start.37 = (f32[256,512]{1,0:T(8,128)}, f32[256,512]{1,0:T(8,128)}, u32[]{:S(2)}, u32[]{:S(2)}) collective-permute-start(f32[256,512]{1,0:T(8,128)} %collective-permute-done.35.a), channel_id=1, source_target_pairs={{0,24},{2,10},{4,28},{6,14},{8,16},{10,2},{12,20},{14,6},{16,8},{1... | collective-permute-start | bytes 1572872 | tf_op jit(solution)/shard_map/ppermute | solution.py:158
  105.6 35.3 %collective-permute-start.26 = (f32[256,512]{1,0:T(8,128)}, f32[256,512]{1,0:T(8,128)}, u32[]{:S(2)}, u32[]{:S(2)}) collective-permute-start(f32[256,512]{1,0:T(8,128)} %shard_map.110.own), channel_id=1, source_target_pairs={{0,24},{2,10},{4,28},{6,14},{8,16},{10,2},{12,20},{14,6},{16,8},{1... | collective-permute-start | bytes 1572872 | tf_op jit(solution)/shard_map/ppermute | solution.py:158
  118.7 21.8 %collective-permute-start.8 = (f32[256,384]{1,0:T(8,128)}, f32[256,384]{1,0:T(8,128)}, u32[]{:S(2)}, u32[]{:S(2)}) collective-permute-start(f32[256,384]{1,0:T(8,128)} %shard_map.101.own), channel_id=1, source_target_pairs={{0,24},{2,10},{4,28},{6,14},{8,16},{10,2},{12,20},{14,6},{16,8},{1... | collective-permute-start | bytes 1179656 | tf_op jit(solution)/shard_map/ppermute | solution.py:158
  123.2 21.4 %collective-permute-start.18 = (f32[256,384]{1,0:T(8,128)}, f32[256,384]{1,0:T(8,128)}, u32[]{:S(2)}, u32[]{:S(2)}) collective-permute-start(f32[256,384]{1,0:T(8,128)} %collective-permute-done.16.a), channel_id=1, source_target_pairs={{0,24},{2,10},{4,28},{6,14},{8,16},{10,2},{12,20},{14,6},{16,8},{1... | collective-permute-start | bytes 1179656 | tf_op jit(solution)/shard_map/ppermute | solution.py:158
  123.2 27.4 %collective-permute-start.27 = (f32[256,512]{1,0:T(8,128)}, f32[256,512]{1,0:T(8,128)}, u32[]{:S(2)}, u32[]{:S(2)}) collective-permute-start(f32[256,512]{1,0:T(8,128)} %collective-permute-done.25.a), channel_id=1, source_target_pairs={{0,24},{2,10},{4,28},{6,14},{8,16},{10,2},{12,20},{14,6},{16,8},{1... | collective-permute-start | bytes 1572872 | tf_op jit(solution)/shard_map/ppermute | solution.py:158
  130.3 19.8 %collective-permute-start.48 = (f32[256,256]{1,0:T(8,128)S(1)}, f32[256,256]{1,0:T(8,128)S(1)}, u32[]{:S(2)}, u32[]{:S(2)}) collective-permute-start(f32[256,256]{1,0:T(8,128)S(1)} %shard_map.119.own), channel_id=1, source_target_pairs={{0,32},{2,98},{4,36},{6,102},{8,40},{10,106},{12,44},{14,110},{16,... | collective-permute-start | bytes 786440 | tf_op jit(solution)/shard_map/ppermute | solution.py:158
  140.4 20.6 %collective-permute-start.38 = (f32[256,512]{1,0:T(8,128)S(1)}, f32[256,512]{1,0:T(8,128)S(1)}, u32[]{:S(2)}, u32[]{:S(2)}) collective-permute-start(f32[256,512]{1,0:T(8,128)S(1)} %shard_map.115.own), channel_id=1, source_target_pairs={{0,32},{2,98},{4,36},{6,102},{8,40},{10,106},{12,44},{14,110},{16,... | collective-permute-start | bytes 1572872 | tf_op jit(solution)/shard_map/ppermute | solution.py:158
  154.1 19.4 %collective-permute-start.28 = (f32[256,512]{1,0:T(8,128)S(1)}, f32[256,512]{1,0:T(8,128)S(1)}, u32[]{:S(2)}, u32[]{:S(2)}) collective-permute-start(f32[256,512]{1,0:T(8,128)S(1)} %shard_map.111.own), channel_id=1, source_target_pairs={{0,32},{2,98},{4,36},{6,102},{8,40},{10,106},{12,44},{14,110},{16,... | collective-permute-start | bytes 1572872 | tf_op jit(solution)/shard_map/ppermute | solution.py:158
  156.7 27.0 %collective-permute-start.39 = (f32[256,512]{1,0:T(8,128)S(1)}, f32[256,512]{1,0:T(8,128)S(1)}, u32[]{:S(2)}, u32[]{:S(2)}) collective-permute-start(f32[256,512]{1,0:T(8,128)S(1)} %shard_map.115.own), channel_id=1, source_target_pairs={{0,96},{2,34},{4,100},{6,38},{8,104},{10,42},{12,108},{14,46},{16,... | collective-permute-start | bytes 1572872 | tf_op jit(solution)/shard_map/ppermute | solution.py:158
  159.8 24.1 %collective-permute-start.29 = (f32[256,512]{1,0:T(8,128)S(1)}, f32[256,512]{1,0:T(8,128)S(1)}, u32[]{:S(2)}, u32[]{:S(2)}) collective-permute-start(f32[256,512]{1,0:T(8,128)S(1)} %shard_map.111.own), channel_id=1, source_target_pairs={{0,96},{2,34},{4,100},{6,38},{8,104},{10,42},{12,108},{14,46},{16,... | collective-permute-start | bytes 1572872 | tf_op jit(solution)/shard_map/ppermute | solution.py:158
  161.0 24.6 %collective-permute-start.40 = (f32[256,512]{1,0:T(8,128)S(1)}, f32[256,512]{1,0:T(8,128)S(1)}, u32[]{:S(2)}, u32[]{:S(2)}) collective-permute-start(f32[256,512]{1,0:T(8,128)S(1)} %collective-permute-done.38.a), channel_id=1, source_target_pairs={{0,96},{2,34},{4,100},{6,38},{8,104},{10,42},{12,108},{14,46},{16,... | collective-permute-start | bytes 1572872 | tf_op jit(solution)/shard_map/ppermute | solution.py:158
  163.6 18.2 %collective-permute-start.10 = (f32[256,384]{1,0:T(8,128)S(1)}, f32[256,384]{1,0:T(8,128)S(1)}, u32[]{:S(2)}, u32[]{:S(2)}) collective-permute-start(f32[256,384]{1,0:T(8,128)S(1)} %shard_map.102.own), channel_id=1, source_target_pairs={{0,32},{2,98},{4,36},{6,102},{8,40},{10,106},{12,44},{14,110},{16,... | collective-permute-start | bytes 1179656 | tf_op jit(solution)/shard_map/ppermute | solution.py:158
  173.4 21.9 %collective-permute-start.30 = (f32[256,512]{1,0:T(8,128)S(1)}, f32[256,512]{1,0:T(8,128)S(1)}, u32[]{:S(2)}, u32[]{:S(2)}) collective-permute-start(f32[256,512]{1,0:T(8,128)S(1)} %collective-permute-done.28.a), channel_id=1, source_target_pairs={{0,96},{2,34},{4,100},{6,38},{8,104},{10,42},{12,108},{14,46},{16,... | collective-permute-start | bytes 1572872 | tf_op jit(solution)/shard_map/ppermute | solution.py:158
  183.6 19.9 %collective-permute-start.11 = (f32[256,384]{1,0:T(8,128)S(1)}, f32[256,384]{1,0:T(8,128)S(1)}, u32[]{:S(2)}, u32[]{:S(2)}) collective-permute-start(f32[256,384]{1,0:T(8,128)S(1)} %shard_map.102.own), channel_id=1, source_target_pairs={{0,96},{2,34},{4,100},{6,38},{8,104},{10,42},{12,108},{14,46},{16,... | collective-permute-start | bytes 1179656 | tf_op jit(solution)/shard_map/ppermute | solution.py:158
  183.9 18.3 %collective-permute-start.21 = (f32[256,384]{1,0:T(8,128)S(1)}, f32[256,384]{1,0:T(8,128)S(1)}, u32[]{:S(2)}, u32[]{:S(2)}) collective-permute-start(f32[256,384]{1,0:T(8,128)S(1)} %collective-permute-done.19.a), channel_id=1, source_target_pairs={{0,96},{2,34},{4,100},{6,38},{8,104},{10,42},{12,108},{14,46},{16,... | collective-permute-start | bytes 1179656 | tf_op jit(solution)/shard_map/ppermute | solution.py:158
  185.7 20.7 %collective-permute-start.12 = (f32[256,384]{1,0:T(8,128)S(1)}, f32[256,384]{1,0:T(8,128)S(1)}, u32[]{:S(2)}, u32[]{:S(2)}) collective-permute-start(f32[256,384]{1,0:T(8,128)S(1)} %collective-permute-done.10.a), channel_id=1, source_target_pairs={{0,96},{2,34},{4,100},{6,38},{8,104},{10,42},{12,108},{14,46},{16,... | collective-permute-start | bytes 1179656 | tf_op jit(solution)/shard_map/ppermute | solution.py:158
  (86 other events, 1052.5 us)
